TPU v7x, 32 devices: a whole 2x2x4 slice. The times are simulated.
32 devices in a mesh: seq: 16 (over z, y, x), head: 2 (over core).
Axes of the slice: x: 2, y: 2, z: 4, core: 2. Of those that a mesh axis runs over, the one named last changes fastest.
Arguments:
- tokens: bfloat16 [16384, 768], P(('seq', 'head')), may hold values from -6 to 6
- documents: int32 [16384], replicated, may hold values from 0 to 15, never falling along the last dimension, each value on 1 to 4096 neighbouring positions
- offsets: int32 [5, 16], P(None, 'head'), may hold values from 0 to 15, as said below
- in_proj: bfloat16 [3, 768, 768], P(None, None, 'head'), may hold values from -0.21875 to 0.21875
- out_proj: bfloat16 [768, 768], P('head'), may hold values from -4 to 4
- up_proj: bfloat16 [768, 3072], P(None, 'head'), may hold values from -0.21875 to 0.21875
- down_proj: bfloat16 [3072, 768], P('head'), may hold values from -0.109375 to 0.109375
- first_gain: float32 [768], replicated, may hold values from 0.25 to 1.75
- first_shift: float32 [768], replicated, may hold values from -3 to 3
- second_gain: float32 [768], replicated, may hold values from 0.25 to 1.75
- second_shift: float32 [768], replicated, may hold values from -3 to 3
- cotangent: bfloat16 [16384, 768], P(('seq', 'head')), may hold values from -6 to 6
Outputs:
- block_out: bfloat16 [16384, 768], P(('seq', 'head'))
- grad_tokens: float32 [16384, 768], P(('seq', 'head'))
- grad_in_proj: float32 [3, 768, 768], P(None, None, 'head')
- grad_out_proj: float32 [768, 768], P('head')
- grad_up_proj: float32 [768, 3072], P(None, 'head')
- grad_down_proj: float32 [3072, 768], P('head')
- grad_first_gain: float32 [768], replicated
- grad_first_shift: float32 [768], replicated
- grad_second_gain: float32 [768], replicated
- grad_second_shift: float32 [768], replicated
Inputs may be any that keep to these rules, and one draw needn't show every extreme that they name: `documents`: slide numbers of the packed tiles never fall; each slide covers 1 to 4096 tiles, one exactly 4096. offsets[b, h] lies in 0 to 2^b - 1; in every branch b some head has offset 2^b - 1.
All inputs are finite; a program needn't handle non-finite values.
Results may differ from a plain program's by a relative error of at most 0.015.
Values may be sent and summed in bfloat16 or wider, within the bound.
A program may use at most 256 MiB of HBM per device.

v0:
```python
import math
from functools import partial

import jax
import jax.numpy as jnp
from jax import lax
from jax.experimental import pallas as pl
from jax.experimental.pallas import tpu as pltpu
from jax.sharding import PartitionSpec as P

E = 48
BRANCHES = 5
SEG0 = 1024
SLOTS = 16
BIT_ROWS = 16
DOC_BITS = 6
ROWS_IN = 3 * E + BIT_ROWS
ROWS_OUT = E + BIT_ROWS
EPS = 1e-05
FAR = 1e30
LOG2E = math.log2(math.e)
LN2 = math.log(2.0)
BF = jnp.bfloat16
F32 = jnp.float32
VMEM_LIMIT = 48 * 2**20


def reversed_bits(value, count):
    out = jnp.zeros_like(value)
    for bit in range(count):
        out = out * 2 + value // 2**bit % 2
    return out


def branch_shape(branch, heads):
    stride = 2**branch
    return (stride, SEG0 // stride, max(1, heads // stride), max(1, stride // heads))


def pieces_of(value):
    high = value.astype(BF).astype(F32)
    rest = value - high
    middle = rest.astype(BF).astype(F32)
    return high, middle, (rest - middle).astype(BF).astype(F32)


def row_block(placed, columns):
    ids = lax.broadcasted_iota(jnp.int32, (BIT_ROWS, columns), 0)
    block = jnp.zeros((BIT_ROWS, columns), F32)
    for row, value in placed.items():
        block = jnp.where(ids == row, value, block)
    return block


def turned_half(block):
    return jnp.concatenate([block[:, 64:], block[:, :64]], axis=1)


def low_half():
    return lax.broadcasted_iota(jnp.int32, (1, 128), 1) < 64


def packed_rows(rows, count):
    return rows if count >= 128 else (rows // 2 + 15) // 16 * 16


def packed(block, half):
    rows = packed_rows(block.shape[0], 64)
    upper, lower = block[:rows], block[block.shape[0] - rows :]
    if isinstance(half, int):
        return jnp.where(low_half(), turned_half(upper) if half else upper, lower if half else turned_half(lower))
    upper = jnp.where(half == 0, upper, turned_half(upper))
    lower = jnp.where(half == 0, turned_half(lower), lower)
    return jnp.where(low_half(), upper, lower)


def unpacked(value, rows, half):
    size = value.shape[0]
    other = turned_half(value)
    upper = jnp.where(half == 0, value, other)
    lower = jnp.where(half == 0, other, value)
    both = jnp.concatenate([upper, lower[2 * size - rows :]], axis=0)
    return jnp.where(low_half() == (half == 0), both, 0.0)


def send_shapes(heads, rows):
    outs = []
    for branch in range(1, BRANCHES):
        stride, count, per, split = branch_shape(branch, heads)
        outs.append(jax.ShapeDtypeStruct((stride, per, packed_rows(rows, count), max(count, 128)), BF))
    return outs


def spread_blocks(heads, head, starts, value, sends):
    for branch in range(1, BRANCHES):
        stride, lanes, per, split = branch_shape(branch, heads)
        send, start = sends[branch - 1], starts[branch, head]
        share = max(1, 128 // lanes)
        span = lanes * share
        block = value[:, :span]
        for part in range(1, SEG0 // span):
            block = jnp.where(start // share == part, value[:, part * span : (part + 1) * span], block)
        if share > 1:
            block = packed(block, start % share)
        block = block.astype(BF)
        if split == 1:
            send[head // per, head % per] = block
        else:
            for copy in range(split):
                send[head * split + copy, 0] = block


def norm_of(values):
    centred = values - jnp.mean(values, axis=-1, keepdims=True)
    scale = lax.rsqrt(jnp.mean(centred * centred, axis=-1, keepdims=True) + EPS)
    return centred * scale, scale


def slot_place(slot):
    return slot % 2 * 8 + slot // 2 % 2 * 4 + slot // 4 % 2 * 2 + slot // 8


def over_slots(body, unroll=4):
    @pl.loop(0, SLOTS // unroll)
    def _(step):
        for part in range(unroll):
            body(step * unroll + part)


def head_copies(source, target, sems, index, scatter):
    size, me = lax.axis_size("head"), lax.axis_index("head")
    copies = []
    for step in range(1, size):
        device = (me + step) % size
        copies.append(
            pltpu.make_async_remote_copy(
                src_ref=source.at[:, device] if scatter else source,
                dst_ref=target.at[step - 1] if scatter else target.at[:, me],
                send_sem=sems.at[0, index, step - 1],
                recv_sem=sems.at[1, index, step - 1],
                device_id={"head": device},
                device_id_type=pl.DeviceIdType.MESH,
            )
        )
    return copies


def load_unit(ref, unit, count, x):
    width = ref.shape[-1]
    if count >= 128:
        for block in range(ref.shape[0]):
            x[:, block * width : (block + 1) * width] = ref[block, unit]
        return
    rows, size = x.shape[0], ref.shape[2]
    for block in range(ref.shape[0] // 2):
        lanes = slice(block * 128, (block + 1) * 128)
        left = ref[2 * block, unit].astype(F32)
        right = ref[2 * block + 1, unit].astype(F32)
        x[:size, lanes] = jnp.where(low_half(), left, turned_half(right)).astype(BF)
        x[rows - size :, lanes] = jnp.where(low_half(), turned_half(left), right).astype(BF)


def store_unit(ref, unit, count, result):
    width = ref.shape[-1]
    for block in range(SEG0 // width):
        value = result[:, block * width : (block + 1) * width]
        if count >= 128:
            ref[block, unit] = value
        else:
            value = value.astype(F32)
            ref[2 * block, unit] = packed(value, 0).astype(BF)
            ref[2 * block + 1, unit] = packed(value, 1).astype(BF)


def forward_unit(x, q_aug, result, base, queries):
    if isinstance(base, int):
        lanes = slice(base, base + queries)
    else:
        lanes = pl.ds(pl.multiple_of(base, 128), queries)
    q_aug[0:E, :queries] = x[0:E, lanes]
    q_aug[E:, :queries] = (x[3 * E :, lanes].astype(F32) * -FAR).astype(BF)
    bits = x[3 * E :, :].astype(F32)
    k_rows = jnp.concatenate([x[E : 2 * E, :], (1.0 - bits).astype(BF)], axis=0).T
    v_aug = jnp.concatenate([x[2 * E : 3 * E, :], jnp.ones(bits.shape, BF)], axis=0)
    if queries < SEG0:
        result[0:E, :] = jnp.zeros((E, SEG0), BF)
        result[E:, :] = row_block({0: -FAR}, SEG0).astype(BF)
    s = jnp.dot(k_rows, q_aug[:, :queries], preferred_element_type=F32)
    top = jnp.max(s, axis=0, keepdims=True)
    p = jnp.exp2(s - top).astype(BF)
    o = jnp.dot(v_aug, p, preferred_element_type=F32)
    total = o[E : E + 1]
    high, middle_part, low = pieces_of(top + jnp.log2(total))
    block = row_block({0: high, 1: middle_part, 2: low}, queries)
    result[:, lanes] = jnp.concatenate([o[:E] * (1.0 / total), block], axis=0).astype(BF)


class Names:
    def __init__(self, refs):
        self.refs = list(refs)

    def take(self, count):
        taken, self.refs = self.refs[:count], self.refs[count:]
        return taken

    def one(self):
        return self.take(1)[0]


def group_place(branch):
    stride = 2**branch
    me = lax.axis_index("seq")
    return me // stride * stride, me % stride


def meet(*axes):
    barrier = pltpu.get_barrier_semaphore()
    count = 0
    for axis in axes:
        size = lax.axis_size(axis)
        me = lax.axis_index(axis)

        @pl.loop(1, size)
        def _(step):
            pl.semaphore_signal(
                barrier, inc=1, device_id={axis: (me + step) % size}, device_id_type=pl.DeviceIdType.MESH
            )

        count += size - 1
    pl.semaphore_wait(barrier, count)


class Reduction:
    STEPS = 7

    def __init__(self, order, total, half, quarter, others, send, recv, begun=False):
        self.total, self.begun = total, begun
        self.half, self.quarter, self.others = half, quarter, others
        self.send, self.recv = send, recv
        me = lax.axis_index("seq")
        self.rest = lax.axis_size("seq") // 4
        self.me = me
        bits = (me % 2, me // 2 % 2)
        self.bits = [bits[bit] for bit in order]
        self.partners = [me + (1 - 2 * bits[bit]) * 2**bit for bit in order]
        self.place = me // 4

    def copy(self, source, target, device, sem):
        return pltpu.make_async_remote_copy(
            src_ref=source,
            dst_ref=target,
            send_sem=self.send.at[sem],
            recv_sem=self.recv.at[sem],
            device_id={"seq": device},
            device_id_type=pl.DeviceIdType.MESH,
        )

    def copies(self, number):
        one, two = self.bits
        rest = self.rest
        others = []
        for step in range(1, rest):
            place = (self.place + step) % rest
            others.append((step, place, place * 4 + self.me % 4))
        if number == 0:
            return [self.copy(self.total.at[1 - one], self.half, self.partners[0], 0)]
        if number == 1:
            return [self.copy(self.half.at[1 - two], self.quarter, self.partners[1], 1)]
        if number == 2:
            return [
                self.copy(self.quarter.at[place], self.others.at[step - 1], device, 1 + step)
                for step, place, device in others
            ]
        if number == 3:
            block = self.total.at[one, two, self.place]
            return [self.copy(block, block, device, rest + step) for step, place, device in others]
        if number == 4:
            block = self.total.at[one, two]
            return [self.copy(block, block, self.partners[1], 2 * rest)]
        if number == 5:
            block = self.total.at[one]
            return [self.copy(block, block, self.partners[0], 2 * rest + 1)]
        return []

    def finish_first(self):
        one, rest = self.bits[0], self.rest
        for copy in self.copies(0):
            copy.wait()

        @pl.loop(0, 2 * rest)
        def _(i):
            j, z = i // rest, i % rest
            mine = self.total[one, j, z].astype(F32)
            self.half[j, z] = (mine + self.half[j, z].astype(F32)).astype(BF)

    def step(self, number):
        one, two = self.bits
        rest = self.rest
        if number == 0 and self.begun:
            return
        if number == 1:
            if not self.begun:
                self.finish_first()
        elif number > 0:
            for copy in self.copies(number - 1):
                copy.wait()
        if number == 2:

            @pl.loop(0, rest)
            def _(z):
                mine = self.half[two, z].astype(F32)
                self.quarter[z] = (mine + self.quarter[z].astype(F32)).astype(BF)

        elif number == 3:
            mine = self.quarter[self.place].astype(F32)
            for step in range(1, rest):
                mine = mine + self.others[step - 1].astype(F32)
            self.total[one, two, self.place] = mine.astype(BF)
        for copy in self.copies(number):
            copy.start()

    @staticmethod
    def scratch(size, rows, columns):
        rest = size // 4
        count = 2 * rest + 2
        return [
            pltpu.VMEM((2, rest, rows, columns), BF),
            pltpu.VMEM((rest, rows, columns), BF),
            pltpu.VMEM((rest - 1, rows, columns), BF),
            pltpu.SemaphoreType.DMA((count,)),
            pltpu.SemaphoreType.DMA((count,)),
        ]


def reduction_parts(value, size):
    rows, columns = value.shape
    return value.reshape(2, 2, size // 4, rows // size, columns)


def reduction_whole(value):
    return value.reshape(-1, value.shape[-1])


def make_reductions(orders, totals, scratch):
    out = []
    for order, total in zip(orders, totals):
        out.append(Reduction(order, total, *scratch[:5]))
        scratch = scratch[5:]
    return out


def group_copies(branch, source, target, send_sems, recv_sems, local_sem):
    stride = 2**branch
    base, place = group_place(branch)
    first = stride - branch - 2
    copies = [
        pltpu.make_async_copy(source.at[place], target.at[place], local_sem.at[branch - 1])
    ]
    for step in range(1, stride):
        member = (place + step) % stride
        copies.append(
            pltpu.make_async_remote_copy(
                src_ref=source.at[member],
                dst_ref=target.at[place],
                send_sem=send_sems.at[first + step],
                recv_sem=recv_sems.at[first + step],
                device_id={"seq": base + member},
                device_id_type=pl.DeviceIdType.MESH,
            )
        )
    return copies


def forward_kernel(heads, starts, tokens, cotangent, bits, scales, in_proj, *refs):
    count = BRANCHES - 1
    names = Names(refs)
    x_rows, normed, cot, own, first = names.take(5)
    gots, backs, outs, sends = names.take(count), names.take(count), names.take(count), names.take(count)
    x, q_aug, result, in_send, in_recv, in_local, out_send, out_recv, out_local = names.take(9)
    spread_rows, normed_own, cot_own, normed_t, head_sems = names.take(5)
    me_head = lax.axis_index("head")
    rows, width = tokens.shape
    per_slot = rows // SLOTS

    def fill(source):
        for column in range(width // 128):
            spread_rows[column] = source[:, column * 128 : (column + 1) * 128].astype(F32)

    def picked(slot):
        at = pl.ds(slot_place(slot), per_slot, stride=SLOTS)
        return jnp.concatenate([spread_rows[column, at, :] for column in range(width // 128)], axis=1)

    fill(tokens)

    @over_slots
    def _(slot):
        value = picked(slot)
        x_rows[pl.ds(pl.multiple_of(slot * per_slot, per_slot), per_slot)] = value
        low = (norm_of(value)[0] * scales[0:1] + scales[1:2]).astype(BF)
        normed_own[slot] = low
        normed[slot, me_head] = low

    meet("seq", "head")
    for copy in head_copies(normed_own, normed, head_sems, 0, False):
        copy.start()
    fill(cotangent)

    @over_slots
    def _(slot):
        low = picked(slot).astype(BF)
        cot_own[slot] = low
        cot[slot, me_head] = low

    for copy in head_copies(cot_own, cot, head_sems, 1, False):
        copy.start()
    own[0, :, 3 * E :, :] = jnp.broadcast_to(bits[...][None], (heads,) + bits.shape)
    turned = [in_proj[j].T for j in range(3)]
    for copy in head_copies(normed_own, normed, head_sems, 0, False):
        copy.wait()
    normed_t[...] = normed[...].reshape(SEG0, width).T
    for j in range(3):
        value = jnp.dot(turned[j], normed_t[...], preferred_element_type=F32)
        if j == 0:
            value = value * (E ** (-0.5) * LOG2E)
        own[0, :, j * E : (j + 1) * E, :] = value.astype(BF).reshape(heads, E, SEG0)

    @pl.loop(0, heads)
    def _(head):
        spread_blocks(heads, head, starts, own[0, head].astype(F32), sends)

    coming = {}
    for branch in range(1, BRANCHES):
        coming[branch] = group_copies(branch, sends[branch - 1], gots[branch - 1], in_send, in_recv, in_local)
        for copy in coming[branch]:
            copy.start()

    @pl.loop(0, heads)
    def _(head):
        x[...] = own[0, head]
        forward_unit(x, q_aug, result, 0, SEG0)
        first[0, head] = result[...]

    leaving = []
    for branch in range(1, BRANCHES):
        stride, lanes, units, split = branch_shape(branch, heads)
        got, out = gots[branch - 1], outs[branch - 1]
        for copy in coming[branch]:
            copy.wait()
        queries = SEG0 // split
        base = 0 if split == 1 else lax.axis_index("seq") % split * queries

        @pl.loop(0, units)
        def _(unit):
            load_unit(got, unit, lanes, x)
            forward_unit(x, q_aug, result, base, queries)
            store_unit(out, unit, lanes, result)

        copies = group_copies(branch, out, backs[branch - 1], out_send, out_recv, out_local)
        for copy in copies:
            copy.start()
        leaving += copies
    for copy in leaving + head_copies(cot_own, cot, head_sems, 1, False):
        copy.wait()


def exchange_scratch():
    copies = 2**BRANCHES - 2 - BRANCHES + 1
    one = [
        pltpu.SemaphoreType.DMA((copies,)),
        pltpu.SemaphoreType.DMA((copies,)),
        pltpu.SemaphoreType.DMA((BRANCHES - 1,)),
    ]
    return one + one


def unit_cost(units, dots):
    return pl.CostEstimate(
        flops=dots * 2 * units * SEG0 * SEG0 * 256,
        transcendentals=units * SEG0 * SEG0,
        bytes_accessed=units * SEG0 * 1000,
    )


def vmem_specs(count):
    return [pl.BlockSpec(memory_space=pltpu.VMEM)] * count


def forward(heads, starts, tokens, cotangent, bits, scales, in_proj):
    head_size = lax.axis_size("head")
    rows, width = tokens.shape
    shard = jax.ShapeDtypeStruct((SLOTS, head_size, rows // SLOTS, width), BF)
    own_rows = pltpu.VMEM((SLOTS, rows // SLOTS, width), BF)
    backs = send_shapes(heads, ROWS_OUT)
    gots = send_shapes(heads, ROWS_IN)
    results = pl.pallas_call(
        partial(forward_kernel, heads),
        in_specs=[pl.BlockSpec(memory_space=pltpu.SMEM)] + vmem_specs(5),
        out_specs=vmem_specs(5 + len(gots) + len(backs)),
        out_shape=[
            jax.ShapeDtypeStruct((rows, width), F32),
            shard,
            shard,
            jax.ShapeDtypeStruct((1, heads, ROWS_IN, SEG0), BF),
            jax.ShapeDtypeStruct((1, heads, ROWS_OUT, SEG0), BF),
        ]
        + gots
        + backs,
        scratch_shapes=[pltpu.VMEM(shape.shape, BF) for shape in backs + gots]
        + [
            pltpu.VMEM((ROWS_IN, SEG0), BF),
            pltpu.VMEM((ROWS_OUT, SEG0), BF),
            pltpu.VMEM((ROWS_OUT, SEG0), BF),
        ]
        + exchange_scratch()
        + [
            pltpu.VMEM((width // 128, rows, 128), F32),
            own_rows,
            own_rows,
            pltpu.VMEM((width, SEG0), BF),
            pltpu.SemaphoreType.DMA((2, 2, head_size - 1)),
        ],
        compiler_params=pltpu.CompilerParams(
            vmem_limit_bytes=60 * 2**20, collective_id=0, has_side_effects=True
        ),
        cost_estimate=unit_cost(2 * heads, 2),
        name="forward",
    )(starts, tokens, cotangent, bits, scales, in_proj)
    return results[:5], results[5 : 5 + len(gots)], results[5 + len(gots) :]


def backward_unit(x, g, q_aug, gk, gv, result, base, queries, tile):
    if isinstance(base, int):
        lanes = slice(base, base + queries)
    else:
        lanes = pl.ds(pl.multiple_of(base, 128), queries)
    extra = g[E:, lanes].astype(F32)
    ids = lax.broadcasted_iota(jnp.int32, extra.shape, 0)
    q = x[0:E, lanes]
    q_aug[0:E, :queries] = q
    q_aug[E:, :queries] = jnp.where(ids >= 12, extra, x[3 * E :, lanes].astype(F32) * -FAR).astype(BF)
    bits = x[3 * E :, :].astype(F32)
    k_aug = jnp.concatenate([x[E : 2 * E, :], (1.0 - bits).astype(BF)], axis=0)
    k_rows = k_aug.T
    v_ids = lax.broadcasted_iota(jnp.int32, bits.shape, 0)
    v_bits = jnp.where(v_ids < 3, 1.0, 0.0).astype(BF)
    v_rows = jnp.concatenate([x[2 * E : 3 * E, :], v_bits], axis=0).T
    q_rows = jnp.concatenate([q, jnp.zeros((BIT_ROWS, queries), BF)], axis=0).T
    g_all = g[:, lanes]
    g_rows = g_all.T
    if queries < SEG0:
        result[0:E, :] = jnp.zeros((E, SEG0), BF)
    for step in range(queries // tile):
        column = step * tile
        span = slice(column, column + tile)
        p = jnp.exp2(jnp.dot(k_rows, q_aug[:, span], preferred_element_type=F32))
        gs = p * jnp.dot(v_rows, g_all[:, span], preferred_element_type=F32)
        p, gs = p.astype(BF), gs.astype(BF)
        target = span if isinstance(base, int) else pl.ds(pl.multiple_of(base + column, 128), tile)
        result[0:E, target] = jnp.dot(k_aug, gs, preferred_element_type=F32)[:E].astype(BF)
        new_k = jnp.dot(gs, q_rows[span], preferred_element_type=F32)
        new_v = jnp.dot(p, g_rows[span], preferred_element_type=F32)
        if step == 0:
            gk[...] = new_k
            gv[...] = new_v
        else:
            gk[...] += new_k
            gv[...] += new_v
    result[E : 2 * E, :] = (gk[...].T[:E] * LN2).astype(BF)
    result[2 * E :, :] = gv[...].T[:E].astype(BF)


ORDERS = {
    'u1': (0, 1), 'u2': (0, 1), 'd1': (1, 0), 'd2': (1, 0), 'o': (0, 1), 'i0': (1, 0), 'i1': (1, 0), 'i2': (0,
    1),
}
EARLY = [
    (0, 'd1', 0), (0, 'u1', 0), (0, 'd1', 1), (0, 'u2', 0), (0, 'u1', 1), (2, 'o', 0), (4, 'u2', 1), (5, 'u1',
    2), (7, 'd1', 2), (9, 'u1', 3), (10, 'd2', 0), (12, 'd2', 1), (12, 'o', 1), (12, 'd1', 3), (13, 'u2', 2),
    (14, 'u1', 4),
]
TAIL = [
    'gather', ('d1', 4), 'in1', ('i1', 0), ('d2', 2), 'in2', ('u2', 3), ('i2', 0), 'in0', ('i0', 0), ('d2',
    3), ('i1', 1), ('i2', 1), ('u1', 5), ('u2', 4), ('d2', 4), ('d1', 5), ('o', 2), ('i2', 2), ('i0', 1),
    ('i1', 2), ('i2', 3), 'one', ('d2', 5), ('o', 3), ('i1', 3), ('u1', 6), ('u2', 5), 'norm', ('i2', 4),
    'gain0', ('i0', 2), ('i1', 4), ('i0', 3), 'gain1', ('o', 4), ('i0', 4), ('i2', 5), 'gain2', ('i1', 5),
    ('o', 5), ('i0', 5), 'gain3', ('i0', 6), ('d2', 6), ('u2', 6), 'gain4', ('d1', 6), ('i1', 6), ('i2', 6),
    ('o', 6),
]


def stream_names(streams):
    pairs = streams // 2
    return [kind + str(i + 1) for i in range(pairs) for kind in "ud"] + ["o"]


def backward_kernel(heads, streams, *refs):
    branches = BRANCHES - 1
    names = Names(refs)
    starts, own, own_g = names.take(3)
    sends, gain, gains_two = names.take(branches), *names.take(2)
    far = names.take(branches + 4)
    parts = names.take(streams)
    up_total, down_total, out_total, in_total = names.take(4)
    chunks = (streams - 1) // 2
    totals = []
    for chunk in range(chunks):
        lanes = pl.ds(chunk * (up_total.shape[-1] // chunks), up_total.shape[-1] // chunks)
        totals += [up_total.at[:, :, :, :, lanes], down_total.at[chunk]]
    totals.append(out_total)
    in_totals = [in_total.at[j] for j in range(3)]
    grad_tokens, gains_out = names.take(2)
    near = names.take(branches + 4)
    units_in, (normed, in_proj, x_rows, grad_hidden) = near[:branches], near[branches:]
    far_sem = names.one()
    first = names.one()
    backs, gots, outs = names.take(branches), names.take(branches), names.take(branches)
    x, g, q_aug, gk, gv, result = names.take(6)
    total, grads, grads_t, normed_t, spread_rows, head_send, head_recv = names.take(7)
    gain_head, gain_one, gain_two, gain_rest = names.take(4)
    in_send, in_recv, in_local, out_send, out_recv, out_local = names.take(6)
    part_sem, head_sems, gain_sems = names.take(3)
    labels = stream_names(streams) + ["i0", "i1", "i2"]
    reductions = make_reductions(
        [ORDERS[label] for label in labels], list(totals) + list(in_totals), names.take(5 * streams + 15)
    )
    reductions = dict(zip(labels, reductions))
    for label in labels[: streams - 1]:
        reductions[label].begun = True

    shapes = [branch_shape(b, heads) for b in range(BRANCHES)]
    size, head_size = lax.axis_size("seq"), lax.axis_size("head")
    me, me_head = lax.axis_index("seq"), lax.axis_index("head")
    rest = size // 4
    tile = 512
    per_slot = x_rows.shape[0] // SLOTS
    width = x_rows.shape[1]

    fills = [
        pltpu.make_async_copy(parts[s], reductions[labels[s]].half, part_sem.at[s]) for s in range(streams - 1)
    ] + [pltpu.make_async_copy(parts[-1], totals[-1], part_sem.at[streams - 1])]
    loads = [pltpu.make_async_copy(far[i], near[i], far_sem.at[i]) for i in range(branches + 4)]
    for copy in fills + loads:
        copy.start()
    meet("seq", "head")

    def coming(branch):
        return group_copies(branch, sends[branch - 1], gots[branch - 1], in_send, in_recv, in_local)

    def leaving(branch):
        return group_copies(branch, outs[branch - 1], backs[branch - 1], out_send, out_recv, out_local)

    for branch in range(1, BRANCHES):
        for copy in coming(branch):
            copy.start()
    for copy in fills + loads:
        copy.wait()

    def split_branch(branch):
        stride, lanes, units, split = shapes[branch]
        queries = SEG0 // split
        for copy in coming(branch):
            copy.wait()
        load_unit(units_in[branch - 1], 0, lanes, x)
        load_unit(gots[branch - 1], 0, lanes, g)
        backward_unit(x, g, q_aug, gk, gv, result, me % split * queries, queries, min(tile, queries))
        store_unit(outs[branch - 1], 0, lanes, result)

    runs, at = [(0, 0, 0, heads // 2)], heads // 2
    split_at = None
    for branch in range(1, BRANCHES):
        if shapes[branch][3] == 1:
            runs.append((branch, at, 0, shapes[branch][2]))
            at += shapes[branch][2]
    split_at = at
    runs.append((0, at, heads // 2, heads - heads // 2))
    blocks = at + heads - heads // 2
    plan = {}
    for block, stream, step in EARLY:
        if stream in labels:
            plan.setdefault(block * blocks // 15, []).append((stream, step))

    @pl.loop(0, blocks)
    def _(block):
        for after, events in plan.items():

            @pl.when(block == after)
            def _(events=events):
                for stream, step in events:
                    reductions[stream].step(step)

        @pl.when(block == split_at)
        def _():
            for branch in range(1, BRANCHES):
                if shapes[branch][3] > 1:
                    split_branch(branch)
                    for copy in leaving(branch):
                        copy.start()

        for branch, low, unit, count in runs:

            @pl.when((block >= low) & (block < low + count))
            def _(branch=branch, low=low, unit=unit):
                if branch == 0:
                    x[...] = own[0, block - low + unit]
                    g[...] = own_g[0, block - low + unit]
                else:

                    @pl.when(block == low)
                    def _():
                        for copy in coming(branch):
                            copy.wait()

                    load_unit(units_in[branch - 1], block - low, shapes[branch][1], x)
                    load_unit(gots[branch - 1], block - low, shapes[branch][1], g)

        backward_unit(x, g, q_aug, gk, gv, result, 0, SEG0, tile)
        for branch, low, unit, count in runs:

            @pl.when((block >= low) & (block < low + count))
            def _(branch=branch, low=low, unit=unit, count=count):
                if branch == 0:
                    first[block - low + unit] = result[...]
                else:
                    store_unit(outs[branch - 1], block - low, shapes[branch][1], result)

                    @pl.when(block == low + count - 1)
                    def _():
                        for copy in leaving(branch):
                            copy.start()

    tasks = {}

    def task(work):
        tasks[work.__name__] = work

    @task
    def gather():
        for branch in range(1, BRANCHES):
            for copy in leaving(branch):
                copy.wait()

        @pl.loop(0, heads)
        def _(head):
            total[...] = first[head].astype(F32)
            for branch in range(1, BRANCHES):
                stride, lanes, per, split = shapes[branch]
                back, start = backs[branch - 1], starts[branch, head]
                if split == 1:
                    value = back[head // per, head % per].astype(F32)
                else:
                    value = back[head * split, 0].astype(F32)
                    for copy in range(1, split):
                        value = value + back[head * split + copy, 0].astype(F32)
                if lanes < 128:
                    value = unpacked(value, 3 * E, start % 2)
                    start = start // 2
                    lanes = 128
                for block in range(SEG0 // lanes):
                    span = slice(block * lanes, (block + 1) * lanes)
                    total[:, span] += jnp.where(start == block, value, 0.0)
            grads[0, head] = (total[0:E, :] * E ** (-0.5)).astype(BF)
            grads[1, head] = total[E : 2 * E, :].astype(BF)
            grads[2, head] = total[2 * E :, :].astype(BF)

        normed_t[...] = normed[...].reshape(SEG0, width).T

    def in_gradient(j):
        rows_in = in_totals[0].shape[3]
        chunk = width // 2
        grads_t[j] = grads[j].reshape(heads * E, SEG0).T
        for half in range(2):
            value = jnp.dot(
                normed_t[half * chunk : (half + 1) * chunk], grads_t[j], preferred_element_type=F32
            ).astype(BF)
            for part in range(chunk // rows_in):
                index = half * (chunk // rows_in) + part
                in_totals[j][index // (2 * rest), index // rest % 2, index % rest] = value[
                    part * rows_in : (part + 1) * rows_in
                ]

    for j in range(3):
        tasks[f"in{j}"] = partial(in_gradient, j)

    def head_swaps():
        swaps = []
        for step in range(1, head_size):
            device = (me_head + step) % head_size
            swaps.append(
                pltpu.make_async_remote_copy(
                    src_ref=head_send.at[device],
                    dst_ref=head_recv.at[step - 1],
                    send_sem=head_sems.at[0, step - 1],
                    recv_sem=head_sems.at[1, step - 1],
                    device_id={"head": device},
                    device_id_type=pl.DeviceIdType.MESH,
                )
            )
        return swaps

    @task
    def one():
        for half in range(2):
            rows = slice(half * SEG0 // 2, (half + 1) * SEG0 // 2)
            value = jnp.zeros((SEG0 // 2, width), F32)
            for j in range(3):
                value = value + lax.dot_general(
                    grads_t[j, rows], in_proj[j], (((1,), (1,)), ((), ())), preferred_element_type=F32
                )
            value = value.astype(BF)
            for slot in range(SLOTS // 2):
                for device in range(head_size):
                    begin = (slot * head_size + device) * per_slot
                    place = (half * SLOTS // 2 + slot) * per_slot
                    head_send[device, place : place + per_slot] = value[begin : begin + per_slot]
        for swap in head_swaps():
            swap.start()

    @task
    def norm():
        for swap in head_swaps():
            swap.wait()
        gain_head[me_head] = jnp.zeros(gains_out.shape, F32)
        gain_head[me_head, 2:4] = gains_two[...]

        @pl.loop(0, SLOTS)
        def _(slot):
            rows = pl.ds(pl.multiple_of(slot * per_slot, per_slot), per_slot)
            grad = head_send[me_head, rows].astype(F32)
            for step in range(1, head_size):
                grad = grad + head_recv[step - 1, rows].astype(F32)
            values = x_rows[rows]
            centred = values - jnp.mean(values, axis=-1, keepdims=True)
            scale = lax.rsqrt(jnp.mean(centred * centred, axis=-1, keepdims=True) + EPS)
            unit = centred * scale
            scaled = grad * gain[0:1]
            inner = jnp.mean(scaled * unit, axis=-1, keepdims=True)
            out = grad_hidden[rows] + scale * (
                scaled - jnp.mean(scaled, axis=-1, keepdims=True) - unit * inner
            )
            place = slot_place(slot)
            for column in range(width // 128):
                lanes = slice(column * 128, (column + 1) * 128)
                spread_rows[column, pl.ds(place, per_slot, stride=SLOTS), :] = out[:, lanes]
            gain_head[me_head, 0:1] += jnp.sum(grad * unit, axis=0, keepdims=True)
            gain_head[me_head, 1:2] += jnp.sum(grad, axis=0, keepdims=True)

        for column in range(width // 128):
            grad_tokens[:, column * 128 : (column + 1) * 128] = spread_rows[column]

    def gain_copy(source, target, axis, device, sem):
        return pltpu.make_async_remote_copy(
            src_ref=source,
            dst_ref=target,
            send_sem=gain_sems.at[0, sem],
            recv_sem=gain_sems.at[1, sem],
            device_id={axis: device},
            device_id_type=pl.DeviceIdType.MESH,
        )

    def gain_copies(stage):
        if stage == 0:
            mine = gain_head.at[me_head]
            return [
                gain_copy(mine, mine, "head", (me_head + step) % head_size, step - 1)
                for step in range(1, head_size)
            ]
        if stage == 1:
            return [gain_copy(gain_one.at[0], gain_one.at[1], "seq", me + 1 - 2 * (me % 2), head_size)]
        if stage == 2:
            device = me + 2 - 4 * (me // 2 % 2)
            return [gain_copy(gain_two.at[0], gain_two.at[1], "seq", device, head_size + 1)]
        spot = me // 4
        block = gain_rest.at[spot]
        return [
            gain_copy(block, block, "seq", (spot + step) % rest * 4 + me % 4, head_size + 1 + step)
            for step in range(1, rest)
        ]

    def summed(ref, count):
        value = ref[0]
        for index in range(1, count):
            value = value + ref[index]
        return value

    def gain_stage(stage):
        if stage > 0:
            for swap in gain_copies(stage - 1):
                swap.wait()
        if stage == 1:
            gain_one[0] = summed(gain_head, head_size)
        elif stage == 2:
            gain_two[0] = summed(gain_one, 2)
        elif stage == 3:
            gain_rest[me // 4] = summed(gain_two, 2)
        elif stage == 4:
            gains_out[...] = summed(gain_rest, rest)
            return
        for swap in gain_copies(stage):
            swap.start()

    for stage in range(5):
        tasks[f"gain{stage}"] = partial(gain_stage, stage)

    for item in TAIL:
        if isinstance(item, str):
            tasks[item]()
        elif item[0] in labels:
            reductions[item[0]].step(item[1])


def backward(heads, starts, own, own_g, units, sends, parts, normed, in_proj, x_rows, grad_hidden, gain, gains_two):
    size, head_size = lax.axis_size("seq"), lax.axis_size("head")
    rest = size // 4
    rows, width = x_rows.shape
    in_shape = (2, 2, rest, width // size, heads * E)
    scratch = []
    for part in parts:
        scratch += Reduction.scratch(size, *part.shape[-2:])
    for _ in range(3):
        scratch += Reduction.scratch(size, *in_shape[-2:])
    streams = len(parts)
    chunks = (streams - 1) // 2
    far = list(units) + [normed, in_proj, x_rows, grad_hidden]
    results = pl.pallas_call(
        partial(backward_kernel, heads, streams),
        in_specs=[pl.BlockSpec(memory_space=pltpu.SMEM)]
        + vmem_specs(2 + len(sends) + 2)
        + [pl.BlockSpec(memory_space=pl.ANY)] * (len(far) + streams),
        out_specs=vmem_specs(6),
        out_shape=[
            jax.ShapeDtypeStruct((2, 2, rest, width // size, chunks * parts[0].shape[-1]), BF),
            jax.ShapeDtypeStruct((chunks, 2, 2, rest) + parts[1].shape[-2:], BF),
            jax.ShapeDtypeStruct(parts[-1].shape, BF),
            jax.ShapeDtypeStruct((3,) + in_shape, BF),
        ]
        + [jax.ShapeDtypeStruct((rows, width), F32), jax.ShapeDtypeStruct((8, width), F32)],
        scratch_shapes=[pltpu.VMEM(value.shape, value.dtype) for value in far]
        + [pltpu.SemaphoreType.DMA((len(far),)), pltpu.VMEM((heads, 3 * E, SEG0), BF)]
        + [pltpu.VMEM(shape.shape, BF) for shape in send_shapes(heads, 3 * E)]
        + [pltpu.VMEM(shape.shape, BF) for shape in send_shapes(heads, ROWS_OUT)]
        + [pltpu.VMEM(shape.shape, BF) for shape in send_shapes(heads, 3 * E)]
        + [
            pltpu.VMEM((ROWS_IN, SEG0), BF),
            pltpu.VMEM((ROWS_OUT, SEG0), BF),
            pltpu.VMEM((ROWS_OUT, SEG0), BF),
            pltpu.VMEM((SEG0, ROWS_OUT), F32),
            pltpu.VMEM((SEG0, ROWS_OUT), F32),
            pltpu.VMEM((3 * E, SEG0), BF),
            pltpu.VMEM((3 * E, SEG0), F32),
            pltpu.VMEM((3, heads, E, SEG0), BF),
            pltpu.VMEM((3, SEG0, heads * E), BF),
            pltpu.VMEM((width, SEG0), BF),
            pltpu.VMEM((width // 128, rows, 128), F32),
            pltpu.VMEM((head_size, rows, width), BF),
            pltpu.VMEM((head_size - 1, rows, width), BF),
            pltpu.VMEM((head_size, 8, width), F32),
            pltpu.VMEM((2, 8, width), F32),
            pltpu.VMEM((2, 8, width), F32),
            pltpu.VMEM((rest, 8, width), F32),
        ]
        + exchange_scratch()
        + [
            pltpu.SemaphoreType.DMA((streams,)),
            pltpu.SemaphoreType.DMA((2, head_size - 1)),
            pltpu.SemaphoreType.DMA((2, head_size + 1 + rest)),
        ]
        + scratch,
        compiler_params=pltpu.CompilerParams(
            vmem_limit_bytes=60 * 2**20, collective_id=1, has_side_effects=True
        ),
        cost_estimate=unit_cost(2 * heads, 5),
        name="backward",
    )(starts, own, own_g, *sends, gain, gains_two, *far, *parts)
    up_total, down_total, out_total, in_total = results[:4]
    sums = [
        up_total.reshape(width, -1).astype(F32),
        down_total.reshape(-1, width).astype(F32),
        out_total.reshape(-1, width).astype(F32),
        in_total.reshape(3, width, heads * E).astype(F32),
    ]
    return sums, results[4], results[5]


def middle_kernel(heads, *refs):
    branches = BRANCHES - 1
    names = Names(refs)
    starts, first = names.take(2)
    backs = names.take(branches)
    scales = names.one()
    far = names.take(5)
    block_out, grad_hidden, gains_two, own_g = names.take(4)
    sends = names.take(branches)
    chunks = max(1, far[3].shape[1] // far[0].shape[1])
    halves = names.take(2 * chunks)
    out_total = names.one()
    merged, lse, mixed, turned, part, got, part_two, got_two = names.take(8)
    hidden_one, normed_own, normed, spread_rows, normed_t, cot_t = names.take(6)
    down_sum, norm_sum, up_grad, down_grad, totals = names.take(5)
    head_sems, first_sems, far_sem = names.take(3)
    near = names.take(5)
    out_proj, x_rows, cot, up, down = near[2], near[0], near[1], near[3], near[4]
    loads = [pltpu.make_async_copy(far[i], near[i], far_sem.at[i]) for i in range(5)]
    for copy in loads:
        copy.start()

    head_size, me_head = lax.axis_size("head"), lax.axis_index("head")
    me = lax.axis_index("seq")
    rest = lax.axis_size("seq") // 4
    width = x_rows.shape[1]
    per_slot = x_rows.shape[0] // SLOTS
    tile = 256

    meet("seq", "head")

    @pl.loop(0, heads)
    def _(head):
        own = first[0, head].astype(F32)
        merged[head] = own[:E]
        lse[head] = own[E : E + 1] + own[E + 1 : E + 2] + own[E + 2 : E + 3]
        for branch in range(1, BRANCHES):
            stride, lanes, per, split = branch_shape(branch, heads)
            back, start = backs[branch - 1], starts[branch, head]
            share = max(1, 128 // lanes)
            for copy in range(split):
                if split == 1:
                    value = back[head // per, head % per].astype(F32)
                else:
                    value = back[head * split + copy, 0].astype(F32)
                if share > 1:
                    value = unpacked(value, ROWS_OUT, start % share)
                new_lse = value[E : E + 1] + value[E + 1 : E + 2] + value[E + 2 : E + 3]
                if share > 1:
                    ids = lax.broadcasted_iota(jnp.int32, new_lse.shape, 1)
                    new_lse = jnp.where(ids // lanes == start % share, new_lse, -FAR)
                span = lanes * share
                for block in range(SEG0 // span):
                    at = slice(block * span, (block + 1) * span)
                    new = jnp.where(start // share == block, new_lse, -FAR)
                    old = lse[head, :, at]
                    top = jnp.maximum(old, new)
                    both = top + jnp.log2(jnp.exp2(old - top) + jnp.exp2(new - top))
                    lse[head, :, at] = both
                    merged[head, :, at] = merged[head, :, at] * jnp.exp2(old - both) + value[:E] * jnp.exp2(
                        new - both
                    )
        mixed[head] = merged[head].astype(BF)

    def rows_of(ref):
        return ref[...].reshape(SEG0, width)

    turned[...] = mixed[...].reshape(heads * E, SEG0).T
    for copy in loads:
        copy.wait()
    for step in range(SEG0 // tile):
        at = slice(step * tile // (head_size * per_slot), (step + 1) * tile // (head_size * per_slot))
        value = jnp.dot(turned[step * tile : (step + 1) * tile], out_proj[...], preferred_element_type=F32)
        part[at] = value.astype(BF).reshape(-1, head_size, per_slot, width)
    for copy in head_copies(part, got, head_sems, 0, True):
        copy.start()
    cot_t[...] = rows_of(cot).T
    for copy in head_copies(part, got, head_sems, 0, True):
        copy.wait()

    def rows_at(slot):
        return pl.ds(pl.multiple_of(slot * per_slot, per_slot), per_slot)

    @over_slots
    def _(slot):
        value = x_rows[rows_at(slot)] + part[slot, me_head].astype(F32)
        for step in range(1, head_size):
            value = value + got[step - 1, slot].astype(F32)
        hidden_one[rows_at(slot)] = value
        unit, scale = norm_of(value)
        low = (unit * scales[2:3] + scales[3:4]).astype(BF)
        normed_own[slot] = low
        normed[slot, me_head] = low

    for copy in head_copies(normed_own, normed, head_sems, 1, False):
        copy.start()
    for copy in head_copies(normed_own, normed, head_sems, 1, False):
        copy.wait()
    normed_t[...] = rows_of(normed).T

    chunk_width = up.shape[1] // chunks
    orders = {0: ORDERS["u1"], 1: ORDERS["d1"]}
    firsts = []
    for chunk in range(chunks):
        for kind in range(2):
            index = 2 * chunk + kind
            firsts.append(
                Reduction(
                    orders[kind], totals.at[index], halves[index], None, None,
                    first_sems.at[0, pl.ds(index, 1)], first_sems.at[1, pl.ds(index, 1)],
                )
            )
    down_sum[...] = jnp.zeros_like(down_sum)
    norm_sum[...] = jnp.zeros_like(norm_sum)
    slots = tile // (head_size * per_slot)
    contract_last = (((1,), (1,)), ((), ()))

    for chunk in range(chunks):
        units = slice(chunk * chunk_width, (chunk + 1) * chunk_width)
        up_grad[...] = jnp.zeros_like(up_grad)
        down_grad[...] = jnp.zeros_like(down_grad)

        @pl.loop(0, SEG0 // tile)
        def _(step):
            rows = pl.ds(pl.multiple_of(step * tile, tile), tile)
            low = normed[pl.ds(step * slots, slots)].reshape(tile, width)
            back = cot[pl.ds(step * slots, slots)].reshape(tile, width)
            pre = jnp.dot(low, up[:, units], preferred_element_type=F32)
            grad = lax.dot_general(back, down[units], contract_last, preferred_element_type=F32)
            share = 0.5 + 0.5 * lax.erf(pre * math.sqrt(0.5))
            density = jnp.exp2(pre * pre * (-0.5 * LOG2E)) * (1.0 / math.sqrt(2.0 * math.pi))
            hidden = (pre * share).astype(BF)
            grad = (grad * (share + pre * density)).astype(BF)
            down_sum[rows] += jnp.dot(hidden, down[units], preferred_element_type=F32)
            norm_sum[rows] += lax.dot_general(grad, up[:, units], contract_last, preferred_element_type=F32)
            up_grad[...] += jnp.dot(normed_t[:, rows], grad, preferred_element_type=F32)
            down_grad[...] += jnp.dot(cot_t[:, rows], hidden, preferred_element_type=F32)

        pieces = totals.shape[3] * 4
        size = totals.shape[4]
        turned_down = down_grad[...].T
        for piece in range(pieces):
            spot = (piece // (2 * rest), piece // rest % 2, piece % rest)
            span = slice(piece * size, (piece + 1) * size)
            totals[(2 * chunk,) + spot] = up_grad[span].astype(BF)
            totals[(2 * chunk + 1,) + spot] = turned_down[span].astype(BF)
        firsts[2 * chunk].step(0)
        firsts[2 * chunk + 1].step(0)

    for ref, value in ((part, down_sum), (part_two, norm_sum)):

        @pl.loop(0, SLOTS)
        def _(slot):
            for device in range(head_size):
                begin = pl.multiple_of((slot * head_size + device) * per_slot, per_slot)
                ref[slot, device] = value[pl.ds(begin, per_slot)].astype(BF)

    for copy in head_copies(part_two, got_two, head_sems, 2, True) + head_copies(part, got, head_sems, 3, True):
        copy.start()
    for copy in head_copies(part_two, got_two, head_sems, 2, True):
        copy.wait()
    gains_two[...] = jnp.zeros_like(gains_two)

    @over_slots
    def _(slot):
        grad = part_two[slot, me_head].astype(F32)
        for step in range(1, head_size):
            grad = grad + got_two[step - 1, slot].astype(F32)
        unit, scale = norm_of(hidden_one[rows_at(slot)])
        scaled = grad * scales[2:3]
        inner = jnp.mean(scaled * unit, axis=-1, keepdims=True)
        out = cot[slot, me_head].astype(F32) + scale * (
            scaled - jnp.mean(scaled, axis=-1, keepdims=True) - unit * inner
        )
        grad_hidden[rows_at(slot)] = out
        normed_own[slot] = out.astype(BF)
        normed[slot, me_head] = out.astype(BF)
        gains_two[0:1] += jnp.sum(grad * unit, axis=0, keepdims=True)
        gains_two[1:2] += jnp.sum(grad, axis=0, keepdims=True)

    for copy in head_copies(normed_own, normed, head_sems, 4, False):
        copy.start()
    for copy in head_copies(part, got, head_sems, 3, True):
        copy.wait()

    @pl.loop(0, SLOTS)
    def _(slot):
        value = hidden_one[rows_at(slot)] + part[slot, me_head].astype(F32)
        for step in range(1, head_size):
            value = value + got[step - 1, slot].astype(F32)
        place = slot_place(slot)
        for column in range(width // 128):
            lanes = slice(column * 128, (column + 1) * 128)
            spread_rows[column, pl.ds(place, per_slot, stride=SLOTS), :] = value[:, lanes]

    for column in range(width // 128):
        block_out[:, column * 128 : (column + 1) * 128] = spread_rows[column].astype(BF)
    for copy in head_copies(normed_own, normed, head_sems, 4, False):
        copy.wait()

    value = jnp.dot(mixed[...].reshape(heads * E, SEG0), rows_of(normed), preferred_element_type=F32)
    size = out_total.shape[3]
    for piece in range(4 * rest):
        spot = (piece // (2 * rest), piece // rest % 2, piece % rest)
        out_total[spot] = value[piece * size : (piece + 1) * size].astype(BF)

    normed_t[...] = rows_of(normed).T
    value = jnp.dot(out_proj[...], normed_t[...], preferred_element_type=F32)
    own_g[0, :, :E, :] = value.astype(BF).reshape(heads, E, SEG0)

    @pl.loop(0, heads)
    def _(head):
        low = own_g[0, head, :E, :]
        dots = jnp.sum(low.astype(F32) * merged[head], axis=0, keepdims=True)
        d = pieces_of(-dots)
        m = pieces_of(-lse[head])
        placed = {0: d[0], 1: d[1], 2: d[2], 12: m[0], 13: m[1], 14: m[2]}
        own_g[0, head, E:, :] = row_block(placed, SEG0).astype(BF)
        own = jnp.concatenate([low.astype(F32), row_block(placed, SEG0)], axis=0)
        spread_blocks(heads, head, starts, own, sends)

    for reduction in firsts:
        reduction.finish_first()


def middle(heads, starts, first, backs, x_rows, cot, out_proj, up, down, scales):
    size, head_size = lax.axis_size("seq"), lax.axis_size("head")
    rest = size // 4
    rows, width = x_rows.shape
    per_slot = rows // SLOTS
    chunks = max(1, up.shape[1] // width)
    shard = (SLOTS, head_size, per_slot, width)
    own = (SLOTS, per_slot, width)
    got = (head_size - 1,) + own
    sends = send_shapes(heads, ROWS_OUT)
    piece = (2, rest, width // size, up.shape[1] // chunks)
    out_piece = (2, 2, rest, heads * E // size, width)
    far = [x_rows, cot, out_proj, up, down]
    results = pl.pallas_call(
        partial(middle_kernel, heads),
        in_specs=[pl.BlockSpec(memory_space=pltpu.SMEM)]
        + vmem_specs(1 + len(backs) + 1)
        + [pl.BlockSpec(memory_space=pl.ANY)] * 5,
        out_specs=vmem_specs(4 + len(sends) + 2 * chunks + 1),
        out_shape=[
            jax.ShapeDtypeStruct((rows, width), BF),
            jax.ShapeDtypeStruct((rows, width), F32),
            jax.ShapeDtypeStruct((2, width), F32),
            jax.ShapeDtypeStruct((1, heads, ROWS_OUT, SEG0), BF),
        ]
        + sends
        + [jax.ShapeDtypeStruct(piece, BF)] * (2 * chunks)
        + [jax.ShapeDtypeStruct(out_piece, BF)],
        scratch_shapes=[
            pltpu.VMEM((heads, E, SEG0), F32),
            pltpu.VMEM((heads, 1, SEG0), F32),
            pltpu.VMEM((heads, E, SEG0), BF),
            pltpu.VMEM((SEG0, heads * E), BF),
            pltpu.VMEM(shard, BF),
            pltpu.VMEM(got, BF),
            pltpu.VMEM(shard, BF),
            pltpu.VMEM(got, BF),
            pltpu.VMEM((rows, width), F32),
            pltpu.VMEM(own, BF),
            pltpu.VMEM(shard, BF),
            pltpu.VMEM((width // 128, rows, 128), F32),
            pltpu.VMEM((width, SEG0), BF),
            pltpu.VMEM((width, SEG0), BF),
            pltpu.VMEM((SEG0, width), F32),
            pltpu.VMEM((SEG0, width), F32),
            pltpu.VMEM((width, up.shape[1] // chunks), F32),
            pltpu.VMEM((width, up.shape[1] // chunks), F32),
            pltpu.VMEM((2 * chunks, 2) + piece, BF),
            pltpu.SemaphoreType.DMA((2, 5, head_size - 1)),
            pltpu.SemaphoreType.DMA((2, 2 * chunks)),
            pltpu.SemaphoreType.DMA((5,)),
        ]
        + [pltpu.VMEM(value.shape, value.dtype) for value in far],
        compiler_params=pltpu.CompilerParams(
            vmem_limit_bytes=60 * 2**20, collective_id=2, has_side_effects=True
        ),
        cost_estimate=pl.CostEstimate(
            flops=14 * SEG0 * width * up.shape[1], transcendentals=0, bytes_accessed=40 * 2**20
        ),
        name="middle",
    )(starts, first, *backs, scales, *far)
    block_out, grad_hidden, gains_two, own_g = results[:4]
    return block_out, grad_hidden, gains_two, own_g, results[4 : 4 + len(sends)], results[4 + len(sends) :]


def local(
    tokens,
    documents,
    offsets,
    in_proj,
    out_proj,
    up_proj,
    down_proj,
    first_gain,
    first_shift,
    second_gain,
    second_shift,
    cotangent,
):
    head_count = lax.axis_size("head")
    seq_id = lax.axis_index("seq")
    row_count = tokens.shape[0]
    seq_len = row_count * head_count
    heads = offsets.shape[1]
    per_slot = row_count // SLOTS

    my_docs = lax.dynamic_slice_in_dim(documents, seq_id * seq_len, seq_len)
    my_docs = my_docs.reshape(head_count, per_slot, 2, 2, 2, 2).transpose(5, 4, 3, 2, 0, 1).reshape(seq_len)
    bit_ids = jnp.arange(BIT_ROWS, dtype=jnp.int32)[:, None]
    doc_bit = my_docs[None, :] // 2 ** (bit_ids % DOC_BITS) % 2
    bits = jnp.where(bit_ids < DOC_BITS, doc_bit, jnp.where(bit_ids < 2 * DOC_BITS, 1 - doc_bit, 0))
    bits = bits.astype(BF)
    starts = jnp.stack([reversed_bits(offsets[b], b) for b in range(BRANCHES)])

    scales = jnp.stack([first_gain, first_shift, second_gain, second_shift])
    (x_rows, normed, cot_all, own, first_out), units, outs = forward(
        heads, starts, tokens, cotangent, bits, scales, in_proj
    )
    block_out, grad_hidden, gains_two, own_g, sends_g, parts = middle(
        heads, starts, first_out, outs, x_rows, cot_all, out_proj, up_proj, down_proj, scales
    )
    (grad_up, grad_down, grad_out, grad_in), grad_tokens, gains = backward(
        heads, starts, own, own_g, units, sends_g, parts,
        normed, in_proj, x_rows, grad_hidden, scales, gains_two,
    )
    return (
        block_out,
        grad_tokens,
        grad_in,
        grad_out,
        grad_up,
        grad_down,
        gains[0],
        gains[1],
        gains[2],
        gains[3],
    )


def solution(mesh):
    placed = (
        P(("seq", "head"), None),
        P(),
        P(None, "head"),
        P(None, None, "head"),
        P("head", None),
        P(None, "head"),
        P("head", None),
        P(),
        P(),
        P(),
        P(),
        P(("seq", "head"), None),
    )
    return jax.shard_map(
        local,
        mesh=mesh,
        in_specs=placed,
        out_specs=(
            P(("seq", "head"), None),
            P(("seq", "head"), None),
            P(None, None, "head"),
            P("head", None),
            P(None, "head"),
            P("head", None),
            P(),
            P(),
            P(),
            P(),
        ),
        check_vma=False,
    )
```

profile of v0, /device:TPU:0, one launch (start us, length us, event | category | flops | bytes accessed | tf_op | source)
XLA Modules:
  0.0 280.5 jit_solution(9660629127770523139)
XLA Ops:
  0.7 0.9 fusion.7
  1.6 0.6 stack.22.starts.refs_0_
  2.2 0.7 stack.23
  2.9 0.7 stack.24
  3.6 0.7 stack.25
  4.2 0.7 stack.26
  4.9 0.6 pad_maximum_fusion.scales.refs_6_.refs_7_
  5.6 0.7 dynamic_slice.3
  6.2 0.4 reshape.125
  6.7 0.2 copy.22
  6.9 0.1 broadcast_in_dim_reshape.3
  7.0 1.4 select_convert_fusion.bits
  8.4 62.8 %forward.1 = (f32[512,768]{1,0:T(8,128)}, bf16[16,2,32,768]{3,2,1,0:T(8,128)(2,1)}, bf16[16,2,32,768]{3,2,1,0:T(8,128)(2,1)}, bf16[1,8,160,1024]{3,2,1,0:T(8,128...) custom-call(s32[5,8]{1,0:T(8,128)} %stack.22.starts.refs_0_, ...), custom_call_target="tpu_custom_call" | custom-call | flops 17179869184 | bytes 16384000 | tf_op jit(solution)/shard_map/forward/pallas_call | solution.py:495
  71.2 53.1 %middle.1 = (bf16[512,768]{1,0:T(8,128)(2,1)}, f32[512,768]{1,0:T(8,128)}, f32[2,768]{1,0:T(2,128)}, bf16[1,8,64,1024]{3,2,1,0:T(8,128)(2,1)}, bf16[2,4,64,512]{...) custom-call(s32[5,8]{1,0:T(8,128)} %stack.22.starts.refs_0_, ...), custom_call_target="tpu_custom_call" | custom-call | flops 16911433728 | bytes 41943040 | tf_op jit(solution)/shard_map/middle/pallas_call | solution.py:1222
  124.3 141.6 %backward.1 = (bf16[2,2,4,48,1536]{4,3,2,1,0:T(8,128)(2,1)}, bf16[2,2,2,4,48,768]{5,4,3,2,1,0:T(8,128)(2,1)}, bf16[2,2,4,24,768]{4,3,2,1,0:T(8,128)(2,1)}, bf16[...) custom-call(s32[5,8]{1,0:T(8,128)} %stack.22.starts.refs_0_, ...), custom_call_target="tpu_custom_call" | custom-call | flops 42949672960 | bytes 16384000 | tf_op jit(solution)/shard_map/backward/pallas_call | solution.py:924
  265.9 0.0 copy-start.2
  265.9 1.6 slice_reduce_fusion
  267.5 2.2 bitcast_convert_fusion.3
  269.6 0.0 copy-done.2
  269.6 0.0 copy-start.1
  269.6 2.2 bitcast_convert_fusion.2
  271.8 0.2 copy-done.1
  272.0 0.0 copy-start
  272.0 3.0 %bitcast_convert_fusion.1 = f32[768,1536]{1,0:T(8,128)} fusion(bf16[2,2,4,48,1536]{4,3,2,1,0:T(8,128)(2,1)S(1)} %copy-done.1), kind=kLoop, calls=%fused_computation.1 | loop fusion | flops 1179648 | bytes 7077888 | tf_op jit(solution)/shard_map/convert_element_type | solution.py:976
  275.0 0.0 copy-done
  275.0 0.0 copy-start.4
  275.0 2.7 bitcast_convert_fusion
  277.7 0.0 copy-done.4
  277.7 0.0 copy-start.3
  277.7 0.9 copy.25
  278.6 0.8 copy-done.3
  279.4 1.1 copy.26
  (4 shorter events, 0.0 us)
Async XLA Ops:
  265.9 3.7 %copy-start.2 = (bf16[3,2,2,4,48,384]{5,4,3,2,1,0:T(8,128)(2,1)S(1)}, bf16[3,2,2,4,48,384]{5,4,3,2,1,0:T(8,128)(2,1)}, u32[]{:S(2)}) copy-start(bf16[3,2,2,4,48,384]{5,4,3,2,1,0:T(8,128)(2,1)} %get-tuple-element.69) | copy-start | bytes 5308420
  269.6 2.4 copy-start.1
  272.0 3.0 %copy-start = (bf16[2,2,2,4,48,768]{5,4,3,2,1,0:T(8,128)(2,1)S(1)}, bf16[2,2,2,4,48,768]{5,4,3,2,1,0:T(8,128)(2,1)}, u32[]{:S(2)}) copy-start(bf16[2,2,2,4,48,768]{5,4,3,2,1,0:T(8,128)(2,1)} %get-tuple-element.72) | copy-start | bytes 7077892
  275.0 2.7 copy-start.4
  277.7 1.7 copy-start.3
where the time goes:
time: 281 us
  Pallas kernels  258 us (92%)
  other arithmetic  12.9 us (5%)
  local copies, waits for them, and re-layouts  9.35 us (3%)
    pallas_call x1, Pallas kernels, backward(): pl.pallas_call(partial(backward_kernel, heads, streams), in_specs=[pl.Blo...  142 us
    pallas_call x1, Pallas kernels, forward(): pl.pallas_call(partial(forward_kernel, heads), in_specs=[pl.BlockSpec(mem...  62.8 us
    pallas_call x1, Pallas kernels, middle(): pl.pallas_call(partial(middle_kernel, heads), in_specs=[pl.BlockSpec(memo...  53.1 us

commit v1 on v0

--- a/solution.py
+++ b/solution.py
@@ -371,13 +371,17 @@
     return copies
 
 
-def forward_kernel(heads, starts, tokens, cotangent, bits, scales, in_proj, *refs):
+def forward_kernel(heads, starts, tokens, cotangent, bits, gain, shift, in_proj, *refs):
     count = BRANCHES - 1
     names = Names(refs)
-    x_rows, normed, cot, own, first = names.take(5)
-    gots, backs, outs, sends = names.take(count), names.take(count), names.take(count), names.take(count)
+    far = names.take(4 + count)
+    first, backs = names.one(), names.take(count)
+    near = names.take(4 + count)
+    (x_rows, normed, cot, own), gots = near[:4], near[4:]
+    outs, sends = names.take(count), names.take(count)
     x, q_aug, result, in_send, in_recv, in_local, out_send, out_recv, out_local = names.take(9)
-    spread_rows, normed_own, cot_own, normed_t, head_sems = names.take(5)
+    spread_rows, normed_own, cot_own, normed_t, head_sems, far_sem = names.take(6)
+    saves = [pltpu.make_async_copy(near[i], far[i], far_sem.at[i]) for i in range(4 + count)]
     me_head = lax.axis_index("head")
     rows, width = tokens.shape
     per_slot = rows // SLOTS
@@ -396,13 +400,14 @@
     def _(slot):
         value = picked(slot)
         x_rows[pl.ds(pl.multiple_of(slot * per_slot, per_slot), per_slot)] = value
-        low = (norm_of(value)[0] * scales[0:1] + scales[1:2]).astype(BF)
+        low = (norm_of(value)[0] * gain[...][None] + shift[...][None]).astype(BF)
         normed_own[slot] = low
         normed[slot, me_head] = low
 
     meet("seq", "head")
     for copy in head_copies(normed_own, normed, head_sems, 0, False):
         copy.start()
+    saves[0].start()
     fill(cotangent)
 
     @over_slots
@@ -423,6 +428,8 @@
         if j == 0:
             value = value * (E ** (-0.5) * LOG2E)
         own[0, :, j * E : (j + 1) * E, :] = value.astype(BF).reshape(heads, E, SEG0)
+    saves[1].start()
+    saves[3].start()
 
     @pl.loop(0, heads)
     def _(head):
@@ -440,12 +447,16 @@
         forward_unit(x, q_aug, result, 0, SEG0)
         first[0, head] = result[...]
 
+    for copy in head_copies(cot_own, cot, head_sems, 1, False):
+        copy.wait()
+    saves[2].start()
     leaving = []
     for branch in range(1, BRANCHES):
         stride, lanes, units, split = branch_shape(branch, heads)
         got, out = gots[branch - 1], outs[branch - 1]
         for copy in coming[branch]:
             copy.wait()
+        saves[3 + branch].start()
         queries = SEG0 // split
         base = 0 if split == 1 else lax.axis_index("seq") % split * queries
 
@@ -459,7 +470,7 @@
         for copy in copies:
             copy.start()
         leaving += copies
-    for copy in leaving + head_copies(cot_own, cot, head_sems, 1, False):
+    for copy in leaving + saves:
         copy.wait()
 
 
@@ -485,27 +496,21 @@
     return [pl.BlockSpec(memory_space=pltpu.VMEM)] * count
 
 
-def forward(heads, starts, tokens, cotangent, bits, scales, in_proj):
+def forward(heads, starts, tokens, cotangent, bits, gain, shift, in_proj):
     head_size = lax.axis_size("head")
     rows, width = tokens.shape
     shard = jax.ShapeDtypeStruct((SLOTS, head_size, rows // SLOTS, width), BF)
     own_rows = pltpu.VMEM((SLOTS, rows // SLOTS, width), BF)
     backs = send_shapes(heads, ROWS_OUT)
     gots = send_shapes(heads, ROWS_IN)
+    own = jax.ShapeDtypeStruct((1, heads, ROWS_IN, SEG0), BF)
+    far = [jax.ShapeDtypeStruct((rows, width), F32), shard, shard, own] + gots
     results = pl.pallas_call(
         partial(forward_kernel, heads),
-        in_specs=[pl.BlockSpec(memory_space=pltpu.SMEM)] + vmem_specs(5),
-        out_specs=vmem_specs(5 + len(gots) + len(backs)),
-        out_shape=[
-            jax.ShapeDtypeStruct((rows, width), F32),
-            shard,
-            shard,
-            jax.ShapeDtypeStruct((1, heads, ROWS_IN, SEG0), BF),
-            jax.ShapeDtypeStruct((1, heads, ROWS_OUT, SEG0), BF),
-        ]
-        + gots
-        + backs,
-        scratch_shapes=[pltpu.VMEM(shape.shape, BF) for shape in backs + gots]
+        in_specs=[pl.BlockSpec(memory_space=pltpu.SMEM)] + vmem_specs(6),
+        out_specs=[pl.BlockSpec(memory_space=pl.ANY)] * len(far) + vmem_specs(1 + len(backs)),
+        out_shape=far + [jax.ShapeDtypeStruct((1, heads, ROWS_OUT, SEG0), BF)] + backs,
+        scratch_shapes=[pltpu.VMEM(shape.shape, shape.dtype) for shape in far + backs + gots]
         + [
             pltpu.VMEM((ROWS_IN, SEG0), BF),
             pltpu.VMEM((ROWS_OUT, SEG0), BF),
@@ -518,14 +523,15 @@
             own_rows,
             pltpu.VMEM((width, SEG0), BF),
             pltpu.SemaphoreType.DMA((2, 2, head_size - 1)),
+            pltpu.SemaphoreType.DMA((len(far),)),
         ],
         compiler_params=pltpu.CompilerParams(
             vmem_limit_bytes=60 * 2**20, collective_id=0, has_side_effects=True
         ),
         cost_estimate=unit_cost(2 * heads, 2),
         name="forward",
-    )(starts, tokens, cotangent, bits, scales, in_proj)
-    return results[:5], results[5 : 5 + len(gots)], results[5 + len(gots) :]
+    )(starts, tokens, cotangent, bits, gain, shift, in_proj)
+    return results[:4], results[4 : len(far)], results[len(far)], results[len(far) + 1 :]
 
 
 def backward_unit(x, g, q_aug, gk, gv, result, base, queries, tile):
@@ -832,7 +838,7 @@
             centred = values - jnp.mean(values, axis=-1, keepdims=True)
             scale = lax.rsqrt(jnp.mean(centred * centred, axis=-1, keepdims=True) + EPS)
             unit = centred * scale
-            scaled = grad * gain[0:1]
+            scaled = grad * gain[...][None]
             inner = jnp.mean(scaled * unit, axis=-1, keepdims=True)
             out = grad_hidden[rows] + scale * (
                 scaled - jnp.mean(scaled, axis=-1, keepdims=True) - unit * inner
@@ -973,12 +979,39 @@
     )(starts, own, own_g, *sends, gain, gains_two, *far, *parts)
     up_total, down_total, out_total, in_total = results[:4]
     sums = [
-        up_total.reshape(width, -1).astype(F32),
-        down_total.reshape(-1, width).astype(F32),
-        out_total.reshape(-1, width).astype(F32),
-        in_total.reshape(3, width, heads * E).astype(F32),
+        in_total.reshape(3, width, heads * E),
+        out_total.reshape(-1, width),
+        up_total.reshape(width, -1),
+        down_total.reshape(-1, width),
     ]
     return sums, results[4], results[5]
+
+
+def finish_kernel(*refs):
+    count = len(refs) // 2
+    for source, target in zip(refs[:count], refs[count:]):
+        target[...] = source[...].astype(target.dtype)
+
+
+def finish(values, types):
+    steps = 8
+    specs = []
+    for value in values:
+        shape = list(value.shape)
+        shape[-2] //= steps
+        if value.ndim == 3:
+            specs.append(pl.BlockSpec(tuple(shape), lambda i: (0, i, 0)))
+        else:
+            specs.append(pl.BlockSpec(tuple(shape), lambda i: (i, 0)))
+    return pl.pallas_call(
+        finish_kernel,
+        grid=(steps,),
+        in_specs=specs,
+        out_specs=specs,
+        out_shape=[jax.ShapeDtypeStruct(value.shape, kind) for value, kind in zip(values, types)],
+        compiler_params=pltpu.CompilerParams(vmem_limit_bytes=61 * 2**20),
+        name="finish",
+    )(*values)
 
 
 def middle_kernel(heads, *refs):
@@ -986,7 +1019,7 @@
     names = Names(refs)
     starts, first = names.take(2)
     backs = names.take(branches)
-    scales = names.one()
+    gain, shift = names.take(2)
     far = names.take(5)
     block_out, grad_hidden, gains_two, own_g = names.take(4)
     sends = names.take(branches)
@@ -1071,7 +1104,7 @@
             value = value + got[step - 1, slot].astype(F32)
         hidden_one[rows_at(slot)] = value
         unit, scale = norm_of(value)
-        low = (unit * scales[2:3] + scales[3:4]).astype(BF)
+        low = (unit * gain[...][None] + shift[...][None]).astype(BF)
         normed_own[slot] = low
         normed[slot, me_head] = low
 
@@ -1150,7 +1183,7 @@
         for step in range(1, head_size):
             grad = grad + got_two[step - 1, slot].astype(F32)
         unit, scale = norm_of(hidden_one[rows_at(slot)])
-        scaled = grad * scales[2:3]
+        scaled = grad * gain[...][None]
         inner = jnp.mean(scaled * unit, axis=-1, keepdims=True)
         out = cot[slot, me_head].astype(F32) + scale * (
             scaled - jnp.mean(scaled, axis=-1, keepdims=True) - unit * inner
@@ -1206,7 +1239,7 @@
         reduction.finish_first()
 
 
-def middle(heads, starts, first, backs, x_rows, cot, out_proj, up, down, scales):
+def middle(heads, starts, first, backs, x_rows, cot, out_proj, up, down, gain, shift):
     size, head_size = lax.axis_size("seq"), lax.axis_size("head")
     rest = size // 4
     rows, width = x_rows.shape
@@ -1222,7 +1255,7 @@
     results = pl.pallas_call(
         partial(middle_kernel, heads),
         in_specs=[pl.BlockSpec(memory_space=pltpu.SMEM)]
-        + vmem_specs(1 + len(backs) + 1)
+        + vmem_specs(1 + len(backs) + 2)
         + [pl.BlockSpec(memory_space=pl.ANY)] * 5,
         out_specs=vmem_specs(4 + len(sends) + 2 * chunks + 1),
         out_shape=[
@@ -1266,7 +1299,7 @@
             flops=14 * SEG0 * width * up.shape[1], transcendentals=0, bytes_accessed=40 * 2**20
         ),
         name="middle",
-    )(starts, first, *backs, scales, *far)
+    )(starts, first, *backs, gain, shift, *far)
     block_out, grad_hidden, gains_two, own_g = results[:4]
     return block_out, grad_hidden, gains_two, own_g, results[4 : 4 + len(sends)], results[4 + len(sends) :]
 
@@ -1300,29 +1333,18 @@
     bits = bits.astype(BF)
     starts = jnp.stack([reversed_bits(offsets[b], b) for b in range(BRANCHES)])
 
-    scales = jnp.stack([first_gain, first_shift, second_gain, second_shift])
-    (x_rows, normed, cot_all, own, first_out), units, outs = forward(
-        heads, starts, tokens, cotangent, bits, scales, in_proj
+    (x_rows, normed, cot_all, own), units, first_out, outs = forward(
+        heads, starts, tokens, cotangent, bits, first_gain, first_shift, in_proj
     )
     block_out, grad_hidden, gains_two, own_g, sends_g, parts = middle(
-        heads, starts, first_out, outs, x_rows, cot_all, out_proj, up_proj, down_proj, scales
+        heads, starts, first_out, outs, x_rows, cot_all, out_proj, up_proj, down_proj, second_gain, second_shift
     )
-    (grad_up, grad_down, grad_out, grad_in), grad_tokens, gains = backward(
+    sums, grad_tokens, gains = backward(
         heads, starts, own, own_g, units, sends_g, parts,
-        normed, in_proj, x_rows, grad_hidden, scales, gains_two,
+        normed, in_proj, x_rows, grad_hidden, first_gain, gains_two,
     )
-    return (
-        block_out,
-        grad_tokens,
-        grad_in,
-        grad_out,
-        grad_up,
-        grad_down,
-        gains[0],
-        gains[1],
-        gains[2],
-        gains[3],
-    )
+    results = finish([block_out, grad_tokens] + sums, [BF] + [F32] * 5)
+    return (*results, gains[0], gains[1], gains[2], gains[3])
 
 
 def solution(mesh):

time: 281 us -> 272 us (0.968)
  other arithmetic: 12.9 us -> 2.29 us
  Pallas kernels: 258 us -> 265 us
  local copies, waits for them, and re-layouts: 9.35 us -> 3.55 us
    pallas_call x0 -> x1, Pallas kernels: none -> 10.7 us  [finish(): pl.pallas_call(finish_kernel, grid=(steps,), in_specs=specs, out_specs=sp...]
    convert_element_type x4 -> x0, other arithmetic: 10 us -> none  [the longest x1 2.98 us: backward(): up_total.reshape(width, -1).astype(F32)]
    pallas_call x1, Pallas kernels: 62.8 us -> 59.8 us  [forward(): pl.pallas_call(partial(forward_kernel, heads), in_specs=[pl.BlockSpec(mem...]
    unnamed x12 -> x0, local copies, waits for them, and re-layouts: 3.02 us -> none
where the time goes in v1:
time: 272 us
  Pallas kernels  265 us (97%)
  local copies, waits for them, and re-layouts  3.55 us (1%)
    pallas_call x1, Pallas kernels, backward(): pl.pallas_call(partial(backward_kernel, heads, streams), in_specs=[pl.Blo...  142 us
    pallas_call x1, Pallas kernels, forward(): pl.pallas_call(partial(forward_kernel, heads), in_specs=[pl.BlockSpec(mem...  59.8 us
    pallas_call x1, Pallas kernels, middle(): pl.pallas_call(partial(middle_kernel, heads), in_specs=[pl.BlockSpec(memo...  53.2 us
    pallas_call x1, Pallas kernels, finish(): pl.pallas_call(finish_kernel, grid=(steps,), in_specs=specs, out_specs=sp...  10.7 us

profile of v1, /device:TPU:0, one launch (start us, length us, event | category | flops | bytes accessed | tf_op | source)
XLA Modules:
  0.0 271.8 jit_solution(5469429502518360179)
XLA Ops:
  0.7 0.9 fusion.7
  1.6 0.6 stack.2.starts.refs_0_
  2.2 0.7 dynamic_slice.3
  2.9 0.4 reshape.125
  3.3 0.2 copy.22
  3.5 0.1 broadcast_in_dim_reshape.3
  3.6 1.4 select_convert_fusion.bits
  5.0 59.8 %forward.1 = (f32[512,768]{1,0:T(8,128)}, bf16[16,2,32,768]{3,2,1,0:T(8,128)(2,1)}, bf16[16,2,32,768]{3,2,1,0:T(8,128)(2,1)}, bf16[1,8,160,1024]{3,2,1,0:T(8,128...) custom-call(s32[5,8]{1,0:T(8,128)} %stack.2.starts.refs_0_, ...), custom_call_target="tpu_custom_call" | custom-call | flops 17179869184 | bytes 16384000 | tf_op jit(solution)/shard_map/forward/pallas_call | solution.py:508
  64.8 53.2 %middle.1 = (bf16[512,768]{1,0:T(8,128)(2,1)}, f32[512,768]{1,0:T(8,128)}, f32[2,768]{1,0:T(2,128)}, bf16[1,8,64,1024]{3,2,1,0:T(8,128)(2,1)}, bf16[2,4,64,512]{...) custom-call(s32[5,8]{1,0:T(8,128)} %stack.2.starts.refs_0_, ...), custom_call_target="tpu_custom_call" | custom-call | flops 16911433728 | bytes 41943040 | tf_op jit(solution)/shard_map/middle/pallas_call | solution.py:1255
  117.9 141.6 %backward.1 = (bf16[2,2,4,48,1536]{4,3,2,1,0:T(8,128)(2,1)}, bf16[2,2,2,4,48,768]{5,4,3,2,1,0:T(8,128)(2,1)}, bf16[2,2,4,24,768]{4,3,2,1,0:T(8,128)(2,1)}, bf16[...) custom-call(s32[5,8]{1,0:T(8,128)} %stack.2.starts.refs_0_, ...), custom_call_target="tpu_custom_call" | custom-call | flops 42949672960 | bytes 16384000 | tf_op jit(solution)/shard_map/backward/pallas_call | solution.py:930
  259.5 1.5 slice_reduce_fusion
  261.0 10.7 %finish.1 = (bf16[512,768]{1,0:T(8,128)(2,1)}, f32[512,768]{1,0:T(8,128)}, f32[3,768,384]{2,1,0:T(8,128)}, f32[384,768]{1,0:T(8,128)}, f32[768,1536]{1,0:T(8,128)}, /*index=5*/f32[1536,768]{1,0:T(8,128)}) custom-call(bf16[512,768]{1,0:T(8,128)(2,1)} %get-tuple-element.55.refs_0_, f32[512,768]{1,0:T(8,128)} %get-tuple-element.74.refs_1_, ...), custom_call_target="tpu_custom_call" | custom-call | tf_op jit(solution)/shard_map/finish/pallas_call | solution.py:1006
  (4 shorter events, 0.0 us)

commit v2 on v1

--- a/solution.py
+++ b/solution.py
@@ -26,8 +26,8 @@
 
 
 def reversed_bits(value, count):
-    out = jnp.zeros_like(value)
-    for bit in range(count):
+    out = value % 2
+    for bit in range(1, count):
         out = out * 2 + value // 2**bit % 2
     return out
 
@@ -91,10 +91,10 @@
     return outs
 
 
-def spread_blocks(heads, head, starts, value, sends):
-    for branch in range(1, BRANCHES):
+def spread_blocks(heads, head, starts, value, sends, branches=range(1, BRANCHES)):
+    for branch in branches:
         stride, lanes, per, split = branch_shape(branch, heads)
-        send, start = sends[branch - 1], starts[branch, head]
+        send, start = sends[branch - 1], reversed_bits(starts[branch, head], branch)
         share = max(1, 128 // lanes)
         span = lanes * share
         block = value[:, :span]
@@ -431,12 +431,13 @@
     saves[1].start()
     saves[3].start()
 
-    @pl.loop(0, heads)
-    def _(head):
-        spread_blocks(heads, head, starts, own[0, head].astype(F32), sends)
-
     coming = {}
     for branch in range(1, BRANCHES):
+
+        @pl.loop(0, heads)
+        def _(head):
+            spread_blocks(heads, head, starts, own[0, head].astype(F32), sends, [branch])
+
         coming[branch] = group_copies(branch, sends[branch - 1], gots[branch - 1], in_send, in_recv, in_local)
         for copy in coming[branch]:
             copy.start()
@@ -602,11 +603,13 @@
 def backward_kernel(heads, streams, *refs):
     branches = BRANCHES - 1
     names = Names(refs)
-    starts, own, own_g = names.take(3)
-    sends, gain, gains_two = names.take(branches), *names.take(2)
-    far = names.take(branches + 4)
+    starts, gain, gains_two = names.take(3)
+    sends = names.take(branches)
+    far = names.take(branches + 6)
     parts = names.take(streams)
-    up_total, down_total, out_total, in_total = names.take(4)
+    far_totals, gains_out = names.take(5), names.one()
+    near_totals, save_sem = names.take(5), names.one()
+    up_total, down_total, out_total, in_total, grad_tokens = near_totals
     chunks = (streams - 1) // 2
     totals = []
     for chunk in range(chunks):
@@ -614,9 +617,8 @@
         totals += [up_total.at[:, :, :, :, lanes], down_total.at[chunk]]
     totals.append(out_total)
     in_totals = [in_total.at[j] for j in range(3)]
-    grad_tokens, gains_out = names.take(2)
-    near = names.take(branches + 4)
-    units_in, (normed, in_proj, x_rows, grad_hidden) = near[:branches], near[branches:]
+    near = names.take(branches + 6)
+    (own, own_g), units_in, (normed, in_proj, x_rows, grad_hidden) = near[:2], near[2:-4], near[-4:]
     far_sem = names.one()
     first = names.one()
     backs, gots, outs = names.take(branches), names.take(branches), names.take(branches)
@@ -644,7 +646,7 @@
     fills = [
         pltpu.make_async_copy(parts[s], reductions[labels[s]].half, part_sem.at[s]) for s in range(streams - 1)
     ] + [pltpu.make_async_copy(parts[-1], totals[-1], part_sem.at[streams - 1])]
-    loads = [pltpu.make_async_copy(far[i], near[i], far_sem.at[i]) for i in range(branches + 4)]
+    loads = [pltpu.make_async_copy(far[i], near[i], far_sem.at[i]) for i in range(branches + 6)]
     for copy in fills + loads:
         copy.start()
     meet("seq", "head")
@@ -734,6 +736,12 @@
                         for copy in leaving(branch):
                             copy.start()
 
+    def saves(index):
+        return pltpu.make_async_copy(near_totals[index], far_totals[index], save_sem.at[index])
+
+    def save(index):
+        saves(index).start()
+
     tasks = {}
 
     def task(work):
@@ -750,7 +758,7 @@
             total[...] = first[head].astype(F32)
             for branch in range(1, BRANCHES):
                 stride, lanes, per, split = shapes[branch]
-                back, start = backs[branch - 1], starts[branch, head]
+                back, start = backs[branch - 1], reversed_bits(starts[branch, head], branch)
                 if split == 1:
                     value = back[head // per, head % per].astype(F32)
                 else:
@@ -852,6 +860,7 @@
 
         for column in range(width // 128):
             grad_tokens[:, column * 128 : (column + 1) * 128] = spread_rows[column]
+        save(4)
 
     def gain_copy(source, target, axis, device, sem):
         return pltpu.make_async_remote_copy(
@@ -907,11 +916,23 @@
     for stage in range(5):
         tasks[f"gain{stage}"] = partial(gain_stage, stage)
 
+    groups = [[], [], ["o"], ["i0", "i1", "i2"]]
+    for chunk in range(chunks):
+        groups[0].append(labels[2 * chunk])
+        groups[1].append(labels[2 * chunk + 1])
     for item in TAIL:
         if isinstance(item, str):
             tasks[item]()
         elif item[0] in labels:
             reductions[item[0]].step(item[1])
+            if item[1] == Reduction.STEPS - 1:
+                for index, group in enumerate(groups):
+                    if item[0] in group:
+                        group.remove(item[0])
+                        if not group:
+                            save(index)
+    for index in range(5):
+        saves(index).wait()
 
 
 def backward(heads, starts, own, own_g, units, sends, parts, normed, in_proj, x_rows, grad_hidden, gain, gains_two):
@@ -926,21 +947,24 @@
         scratch += Reduction.scratch(size, *in_shape[-2:])
     streams = len(parts)
     chunks = (streams - 1) // 2
-    far = list(units) + [normed, in_proj, x_rows, grad_hidden]
+    far = [own, own_g] + list(units) + [normed, in_proj, x_rows, grad_hidden]
+    totals = [
+        jax.ShapeDtypeStruct((2, 2, rest, width // size, chunks * parts[0].shape[-1]), BF),
+        jax.ShapeDtypeStruct((chunks, 2, 2, rest) + parts[1].shape[-2:], BF),
+        jax.ShapeDtypeStruct(parts[-1].shape, BF),
+        jax.ShapeDtypeStruct((3,) + in_shape, BF),
+        jax.ShapeDtypeStruct((rows, width), F32),
+    ]
     results = pl.pallas_call(
         partial(backward_kernel, heads, streams),
         in_specs=[pl.BlockSpec(memory_space=pltpu.SMEM)]
-        + vmem_specs(2 + len(sends) + 2)
-        + [pl.BlockSpec(memory_space=pl.ANY)] * (len(far) + streams),
-        out_specs=vmem_specs(6),
-        out_shape=[
-            jax.ShapeDtypeStruct((2, 2, rest, width // size, chunks * parts[0].shape[-1]), BF),
-            jax.ShapeDtypeStruct((chunks, 2, 2, rest) + parts[1].shape[-2:], BF),
-            jax.ShapeDtypeStruct(parts[-1].shape, BF),
-            jax.ShapeDtypeStruct((3,) + in_shape, BF),
-        ]
-        + [jax.ShapeDtypeStruct((rows, width), F32), jax.ShapeDtypeStruct((8, width), F32)],
-        scratch_shapes=[pltpu.VMEM(value.shape, value.dtype) for value in far]
+        + vmem_specs(2)
+        + [pl.BlockSpec(memory_space=pl.ANY)] * (len(sends) + len(far) + streams),
+        out_specs=[pl.BlockSpec(memory_space=pl.ANY)] * len(totals) + vmem_specs(1),
+        out_shape=totals + [jax.ShapeDtypeStruct((8, width), F32)],
+        scratch_shapes=[pltpu.VMEM(value.shape, value.dtype) for value in totals]
+        + [pltpu.SemaphoreType.DMA((len(totals),))]
+        + [pltpu.VMEM(value.shape, value.dtype) for value in far]
         + [pltpu.SemaphoreType.DMA((len(far),)), pltpu.VMEM((heads, 3 * E, SEG0), BF)]
         + [pltpu.VMEM(shape.shape, BF) for shape in send_shapes(heads, 3 * E)]
         + [pltpu.VMEM(shape.shape, BF) for shape in send_shapes(heads, ROWS_OUT)]
@@ -976,7 +1000,7 @@
         ),
         cost_estimate=unit_cost(2 * heads, 5),
         name="backward",
-    )(starts, own, own_g, *sends, gain, gains_two, *far, *parts)
+    )(starts, gain, gains_two, *sends, *far, *parts)
     up_total, down_total, out_total, in_total = results[:4]
     sums = [
         in_total.reshape(3, width, heads * E),
@@ -1027,7 +1051,7 @@
     halves = names.take(2 * chunks)
     out_total = names.one()
     merged, lse, mixed, turned, part, got, part_two, got_two = names.take(8)
-    hidden_one, normed_own, normed, spread_rows, normed_t, cot_t = names.take(6)
+    hidden_one, normed_own, normed, spread_rows, normed_t = names.take(5)
     down_sum, norm_sum, up_grad, down_grad, totals = names.take(5)
     head_sems, first_sems, far_sem = names.take(3)
     near = names.take(5)
@@ -1052,7 +1076,7 @@
         lse[head] = own[E : E + 1] + own[E + 1 : E + 2] + own[E + 2 : E + 3]
         for branch in range(1, BRANCHES):
             stride, lanes, per, split = branch_shape(branch, heads)
-            back, start = backs[branch - 1], starts[branch, head]
+            back, start = backs[branch - 1], reversed_bits(starts[branch, head], branch)
             share = max(1, 128 // lanes)
             for copy in range(split):
                 if split == 1:
@@ -1090,7 +1114,6 @@
         part[at] = value.astype(BF).reshape(-1, head_size, per_slot, width)
     for copy in head_copies(part, got, head_sems, 0, True):
         copy.start()
-    cot_t[...] = rows_of(cot).T
     for copy in head_copies(part, got, head_sems, 0, True):
         copy.wait()
 
@@ -1150,16 +1173,15 @@
             down_sum[rows] += jnp.dot(hidden, down[units], preferred_element_type=F32)
             norm_sum[rows] += lax.dot_general(grad, up[:, units], contract_last, preferred_element_type=F32)
             up_grad[...] += jnp.dot(normed_t[:, rows], grad, preferred_element_type=F32)
-            down_grad[...] += jnp.dot(cot_t[:, rows], hidden, preferred_element_type=F32)
+            down_grad[...] += jnp.dot(hidden.T, back, preferred_element_type=F32)
 
         pieces = totals.shape[3] * 4
         size = totals.shape[4]
-        turned_down = down_grad[...].T
         for piece in range(pieces):
             spot = (piece // (2 * rest), piece // rest % 2, piece % rest)
             span = slice(piece * size, (piece + 1) * size)
             totals[(2 * chunk,) + spot] = up_grad[span].astype(BF)
-            totals[(2 * chunk + 1,) + spot] = turned_down[span].astype(BF)
+            totals[(2 * chunk + 1,) + spot] = down_grad[span].astype(BF)
         firsts[2 * chunk].step(0)
         firsts[2 * chunk + 1].step(0)
 
@@ -1281,11 +1303,10 @@
             pltpu.VMEM(shard, BF),
             pltpu.VMEM((width // 128, rows, 128), F32),
             pltpu.VMEM((width, SEG0), BF),
-            pltpu.VMEM((width, SEG0), BF),
             pltpu.VMEM((SEG0, width), F32),
             pltpu.VMEM((SEG0, width), F32),
             pltpu.VMEM((width, up.shape[1] // chunks), F32),
-            pltpu.VMEM((width, up.shape[1] // chunks), F32),
+            pltpu.VMEM((up.shape[1] // chunks, width), F32),
             pltpu.VMEM((2 * chunks, 2) + piece, BF),
             pltpu.SemaphoreType.DMA((2, 5, head_size - 1)),
             pltpu.SemaphoreType.DMA((2, 2 * chunks)),
@@ -1331,16 +1352,15 @@
     doc_bit = my_docs[None, :] // 2 ** (bit_ids % DOC_BITS) % 2
     bits = jnp.where(bit_ids < DOC_BITS, doc_bit, jnp.where(bit_ids < 2 * DOC_BITS, 1 - doc_bit, 0))
     bits = bits.astype(BF)
-    starts = jnp.stack([reversed_bits(offsets[b], b) for b in range(BRANCHES)])
 
     (x_rows, normed, cot_all, own), units, first_out, outs = forward(
-        heads, starts, tokens, cotangent, bits, first_gain, first_shift, in_proj
+        heads, offsets, tokens, cotangent, bits, first_gain, first_shift, in_proj
     )
     block_out, grad_hidden, gains_two, own_g, sends_g, parts = middle(
-        heads, starts, first_out, outs, x_rows, cot_all, out_proj, up_proj, down_proj, second_gain, second_shift
+        heads, offsets, first_out, outs, x_rows, cot_all, out_proj, up_proj, down_proj, second_gain, second_shift
     )
     sums, grad_tokens, gains = backward(
-        heads, starts, own, own_g, units, sends_g, parts,
+        heads, offsets, own, own_g, units, sends_g, parts,
         normed, in_proj, x_rows, grad_hidden, first_gain, gains_two,
     )
     results = finish([block_out, grad_tokens] + sums, [BF] + [F32] * 5)

time: 272 us -> 267 us (0.982)
  Pallas kernels: 265 us -> 262 us
where the time goes in v2:
time: 267 us
  Pallas kernels  262 us (98%)
  local copies, waits for them, and re-layouts  2.94 us (1%)
    pallas_call x1, Pallas kernels, backward(): pl.pallas_call(partial(backward_kernel, heads, streams), in_specs=[pl.Blo...  139 us
    pallas_call x1, Pallas kernels, forward(): pl.pallas_call(partial(forward_kernel, heads), in_specs=[pl.BlockSpec(mem...  58.7 us
    pallas_call x1, Pallas kernels, middle(): pl.pallas_call(partial(middle_kernel, heads), in_specs=[pl.BlockSpec(memo...  53 us
    pallas_call x1, Pallas kernels, finish(): pl.pallas_call(finish_kernel, grid=(steps,), in_specs=specs, out_specs=sp...  10.7 us

profile of v2, /device:TPU:0, one launch (start us, length us, event | category | flops | bytes accessed | tf_op | source)
XLA Modules:
  0.0 266.9 jit_solution(129982800281319959)
XLA Ops:
  0.7 0.7 dynamic_slice.3
  1.4 0.4 reshape.125
  1.8 0.2 copy.22
  2.0 0.1 broadcast_in_dim_reshape.3
  2.1 1.4 select_convert_fusion.bits
  3.5 58.7 %forward.1 = (f32[512,768]{1,0:T(8,128)}, bf16[16,2,32,768]{3,2,1,0:T(8,128)(2,1)}, bf16[16,2,32,768]{3,2,1,0:T(8,128)(2,1)}, bf16[1,8,160,1024]{3,2,1,0:T(8,128...) custom-call(s32[5,8]{1,0:T(8,128)} %refs_0_.3, ...), custom_call_target="tpu_custom_call" | custom-call | flops 17179869184 | bytes 16384000 | tf_op jit(solution)/shard_map/forward/pallas_call | solution.py:509
  62.2 53.0 %middle.1 = (bf16[512,768]{1,0:T(8,128)(2,1)}, f32[512,768]{1,0:T(8,128)}, f32[2,768]{1,0:T(2,128)}, bf16[1,8,64,1024]{3,2,1,0:T(8,128)(2,1)}, bf16[2,4,64,512]{...) custom-call(s32[5,8]{1,0:T(8,128)} %refs_0_.3, ...), custom_call_target="tpu_custom_call" | custom-call | flops 16911433728 | bytes 41943040 | tf_op jit(solution)/shard_map/middle/pallas_call | solution.py:1277
  115.3 139.3 %backward.1 = (bf16[2,2,4,48,1536]{4,3,2,1,0:T(8,128)(2,1)}, bf16[2,2,2,4,48,768]{5,4,3,2,1,0:T(8,128)(2,1)}, bf16[2,2,4,24,768]{4,3,2,1,0:T(8,128)(2,1)}, bf16[...) custom-call(s32[5,8]{1,0:T(8,128)} %refs_0_.3, f32[768]{0:T(1024)} %refs_1_.1, ...), custom_call_target="tpu_custom_call" | custom-call | flops 42949672960 | bytes 16384000 | tf_op jit(solution)/shard_map/backward/pallas_call | solution.py:958
  254.6 1.5 slice_reduce_fusion
  256.1 10.7 %finish.1 = (bf16[512,768]{1,0:T(8,128)(2,1)}, f32[512,768]{1,0:T(8,128)}, f32[3,768,384]{2,1,0:T(8,128)}, f32[384,768]{1,0:T(8,128)}, f32[768,1536]{1,0:T(8,128)}, /*index=5*/f32[1536,768]{1,0:T(8,128)}) custom-call(bf16[512,768]{1,0:T(8,128)(2,1)} %get-tuple-element.55.refs_0_, f32[512,768]{1,0:T(8,128)} %get-tuple-element.74.refs_1_, ...), custom_call_target="tpu_custom_call" | custom-call | tf_op jit(solution)/shard_map/finish/pallas_call | solution.py:1030
  (3 shorter events, 0.0 us)

commit v3 on v2

--- a/solution.py
+++ b/solution.py
@@ -643,12 +643,18 @@
     per_slot = x_rows.shape[0] // SLOTS
     width = x_rows.shape[1]
 
-    fills = [
-        pltpu.make_async_copy(parts[s], reductions[labels[s]].half, part_sem.at[s]) for s in range(streams - 1)
-    ] + [pltpu.make_async_copy(parts[-1], totals[-1], part_sem.at[streams - 1])]
-    loads = [pltpu.make_async_copy(far[i], near[i], far_sem.at[i]) for i in range(branches + 6)]
-    for copy in fills + loads:
-        copy.start()
+
+    def fill(s):
+        target = reductions[labels[s]].half if s < streams - 1 else totals[-1]
+        return pltpu.make_async_copy(parts[s], target, part_sem.at[s])
+
+    def load(i):
+        return pltpu.make_async_copy(far[i], near[i], far_sem.at[i])
+
+    for s in range(streams):
+        fill(s).start()
+    for i in range(branches + 6):
+        load(i).start()
     meet("seq", "head")
 
     def coming(branch):
@@ -660,12 +666,18 @@
     for branch in range(1, BRANCHES):
         for copy in coming(branch):
             copy.start()
-    for copy in fills + loads:
-        copy.wait()
+    for i in range(2):
+        load(i).wait()
+
+    def advance(label, number):
+        if label in labels[:streams] and number == (1 if reductions[label].begun else 0):
+            fill(labels.index(label)).wait()
+        reductions[label].step(number)
 
     def split_branch(branch):
         stride, lanes, units, split = shapes[branch]
         queries = SEG0 // split
+        load(1 + branch).wait()
         for copy in coming(branch):
             copy.wait()
         load_unit(units_in[branch - 1], 0, lanes, x)
@@ -694,7 +706,7 @@
             @pl.when(block == after)
             def _(events=events):
                 for stream, step in events:
-                    reductions[stream].step(step)
+                    advance(stream, step)
 
         @pl.when(block == split_at)
         def _():
@@ -715,6 +727,7 @@
 
                     @pl.when(block == low)
                     def _():
+                        load(1 + branch).wait()
                         for copy in coming(branch):
                             copy.wait()
 
@@ -749,6 +762,8 @@
 
     @task
     def gather():
+        for i in range(4):
+            load(branches + 2 + i).wait()
         for branch in range(1, BRANCHES):
             for copy in leaving(branch):
                 copy.wait()
@@ -924,7 +939,7 @@
         if isinstance(item, str):
             tasks[item]()
         elif item[0] in labels:
-            reductions[item[0]].step(item[1])
+            advance(item[0], item[1])
             if item[1] == Reduction.STEPS - 1:
                 for index, group in enumerate(groups):
                     if item[0] in group:
@@ -1018,7 +1033,7 @@
 
 
 def finish(values, types):
-    steps = 8
+    steps = 2
     specs = []
     for value in values:
         shape = list(value.shape)
@@ -1057,8 +1072,8 @@
     near = names.take(5)
     out_proj, x_rows, cot, up, down = near[2], near[0], near[1], near[3], near[4]
     loads = [pltpu.make_async_copy(far[i], near[i], far_sem.at[i]) for i in range(5)]
-    for copy in loads:
-        copy.start()
+    for i in (2, 0, 1, 3, 4):
+        loads[i].start()
 
     head_size, me_head = lax.axis_size("head"), lax.axis_index("head")
     me = lax.axis_index("seq")
@@ -1106,14 +1121,16 @@
         return ref[...].reshape(SEG0, width)
 
     turned[...] = mixed[...].reshape(heads * E, SEG0).T
-    for copy in loads:
-        copy.wait()
+    loads[2].wait()
     for step in range(SEG0 // tile):
         at = slice(step * tile // (head_size * per_slot), (step + 1) * tile // (head_size * per_slot))
         value = jnp.dot(turned[step * tile : (step + 1) * tile], out_proj[...], preferred_element_type=F32)
         part[at] = value.astype(BF).reshape(-1, head_size, per_slot, width)
     for copy in head_copies(part, got, head_sems, 0, True):
         copy.start()
+    for ref in (down_sum, norm_sum, up_grad, down_grad):
+        ref[...] = jnp.zeros_like(ref)
+    loads[0].wait()
     for copy in head_copies(part, got, head_sems, 0, True):
         copy.wait()
 
@@ -1136,6 +1153,8 @@
     for copy in head_copies(normed_own, normed, head_sems, 1, False):
         copy.wait()
     normed_t[...] = rows_of(normed).T
+    for i in (1, 3, 4):
+        loads[i].wait()
 
     chunk_width = up.shape[1] // chunks
     orders = {0: ORDERS["u1"], 1: ORDERS["d1"]}
@@ -1149,15 +1168,14 @@
                     first_sems.at[0, pl.ds(index, 1)], first_sems.at[1, pl.ds(index, 1)],
                 )
             )
-    down_sum[...] = jnp.zeros_like(down_sum)
-    norm_sum[...] = jnp.zeros_like(norm_sum)
     slots = tile // (head_size * per_slot)
     contract_last = (((1,), (1,)), ((), ()))
 
     for chunk in range(chunks):
         units = slice(chunk * chunk_width, (chunk + 1) * chunk_width)
-        up_grad[...] = jnp.zeros_like(up_grad)
-        down_grad[...] = jnp.zeros_like(down_grad)
+        if chunk > 0:
+            up_grad[...] = jnp.zeros_like(up_grad)
+            down_grad[...] = jnp.zeros_like(down_grad)
 
         @pl.loop(0, SEG0 // tile)
         def _(step):

time: 267 us -> 263 us (0.985)
  Pallas kernels: 262 us -> 257 us
where the time goes in v3:
time: 263 us; the launch traced here: 262 us
  Pallas kernels  257 us (98%)
  local copies, waits for them, and re-layouts  2.94 us (1%)
    pallas_call x1, Pallas kernels, backward(): pl.pallas_call(partial(backward_kernel, heads, streams), in_specs=[pl.Blo...  138 us
    pallas_call x1, Pallas kernels, forward(): pl.pallas_call(partial(forward_kernel, heads), in_specs=[pl.BlockSpec(mem...  58.7 us
    pallas_call x1, Pallas kernels, middle(): pl.pallas_call(partial(middle_kernel, heads), in_specs=[pl.BlockSpec(memo...  52.2 us
    pallas_call x1, Pallas kernels, finish(): pl.pallas_call(finish_kernel, grid=(steps,), in_specs=specs, out_specs=sp...  8.59 us

profile of v3, /device:TPU:0, one launch (start us, length us, event | category | flops | bytes accessed | tf_op | source)
XLA Modules:
  0.0 262.3 jit_solution(4143683141041768918)
XLA Ops:
  0.7 0.7 dynamic_slice.3
  1.4 0.4 reshape.125
  1.8 0.2 copy.22
  2.0 0.1 broadcast_in_dim_reshape.3
  2.1 1.4 select_convert_fusion.bits
  3.5 58.7 %forward.1 = (f32[512,768]{1,0:T(8,128)}, bf16[16,2,32,768]{3,2,1,0:T(8,128)(2,1)}, bf16[16,2,32,768]{3,2,1,0:T(8,128)(2,1)}, bf16[1,8,160,1024]{3,2,1,0:T(8,128...) custom-call(s32[5,8]{1,0:T(8,128)} %refs_0_.3, ...), custom_call_target="tpu_custom_call" | custom-call | flops 17179869184 | bytes 16384000 | tf_op jit(solution)/shard_map/forward/pallas_call | solution.py:509
  62.2 52.2 %middle.1 = (bf16[512,768]{1,0:T(8,128)(2,1)}, f32[512,768]{1,0:T(8,128)}, f32[2,768]{1,0:T(2,128)}, bf16[1,8,64,1024]{3,2,1,0:T(8,128)(2,1)}, bf16[2,4,64,512]{...) custom-call(s32[5,8]{1,0:T(8,128)} %refs_0_.3, ...), custom_call_target="tpu_custom_call" | custom-call | flops 16911433728 | bytes 41943040 | tf_op jit(solution)/shard_map/middle/pallas_call | solution.py:1295
  114.4 137.7 %backward.1 = (bf16[2,2,4,48,1536]{4,3,2,1,0:T(8,128)(2,1)}, bf16[2,2,2,4,48,768]{5,4,3,2,1,0:T(8,128)(2,1)}, bf16[2,2,4,24,768]{4,3,2,1,0:T(8,128)(2,1)}, bf16[...) custom-call(s32[5,8]{1,0:T(8,128)} %refs_0_.3, f32[768]{0:T(1024)} %refs_1_.1, ...), custom_call_target="tpu_custom_call" | custom-call | flops 42949672960 | bytes 16384000 | tf_op jit(solution)/shard_map/backward/pallas_call | solution.py:973
  252.2 1.5 slice_reduce_fusion
  253.7 8.6 %finish.1 = (bf16[512,768]{1,0:T(8,128)(2,1)}, f32[512,768]{1,0:T(8,128)}, f32[3,768,384]{2,1,0:T(8,128)}, f32[384,768]{1,0:T(8,128)}, f32[768,1536]{1,0:T(8,128)}, /*index=5*/f32[1536,768]{1,0:T(8,128)}) custom-call(bf16[512,768]{1,0:T(8,128)(2,1)} %get-tuple-element.55.refs_0_, f32[512,768]{1,0:T(8,128)} %get-tuple-element.74.refs_1_, ...), custom_call_target="tpu_custom_call" | custom-call | tf_op jit(solution)/shard_map/finish/pallas_call | solution.py:1045
  (3 shorter events, 0.0 us)

commit v4 on v3

--- a/solution.py
+++ b/solution.py
@@ -1026,13 +1026,15 @@
     return sums, results[4], results[5]
 
 
-def finish_kernel(*refs):
-    count = len(refs) // 2
-    for source, target in zip(refs[:count], refs[count:]):
+def finish_kernel(gains, *refs):
+    count = (len(refs) - 4) // 2
+    for source, target in zip(refs[:count], refs[count : 2 * count]):
         target[...] = source[...].astype(target.dtype)
-
-
-def finish(values, types):
+    for index in range(4):
+        refs[2 * count + index][...] = gains[index]
+
+
+def finish(values, types, gains):
     steps = 2
     specs = []
     for value in values:
@@ -1045,12 +1047,13 @@
     return pl.pallas_call(
         finish_kernel,
         grid=(steps,),
-        in_specs=specs,
-        out_specs=specs,
-        out_shape=[jax.ShapeDtypeStruct(value.shape, kind) for value, kind in zip(values, types)],
+        in_specs=[pl.BlockSpec(gains.shape, lambda i: (0, 0))] + specs,
+        out_specs=specs + [pl.BlockSpec(gains.shape[1:], lambda i: (0,))] * 4,
+        out_shape=[jax.ShapeDtypeStruct(value.shape, kind) for value, kind in zip(values, types)]
+        + [jax.ShapeDtypeStruct(gains.shape[1:], F32)] * 4,
         compiler_params=pltpu.CompilerParams(vmem_limit_bytes=61 * 2**20),
         name="finish",
-    )(*values)
+    )(gains, *values)
 
 
 def middle_kernel(heads, *refs):
@@ -1060,11 +1063,13 @@
     backs = names.take(branches)
     gain, shift = names.take(2)
     far = names.take(5)
-    block_out, grad_hidden, gains_two, own_g = names.take(4)
-    sends = names.take(branches)
     chunks = max(1, far[3].shape[1] // far[0].shape[1])
-    halves = names.take(2 * chunks)
-    out_total = names.one()
+    saved = 4 + branches + 2 * chunks
+    far_results, gains_two = names.take(saved), names.one()
+    near_results, save_sem = names.take(saved), names.one()
+    block_out, grad_hidden, own_g, out_total = near_results[:4]
+    sends, halves = near_results[4 : 4 + branches], near_results[4 + branches :]
+    saves = [pltpu.make_async_copy(near_results[i], far_results[i], save_sem.at[i]) for i in range(saved)]
     merged, lse, mixed, turned, part, got, part_two, got_two = names.take(8)
     hidden_one, normed_own, normed, spread_rows, normed_t = names.take(5)
     down_sum, norm_sum, up_grad, down_grad, totals = names.take(5)
@@ -1236,6 +1241,7 @@
 
     for copy in head_copies(normed_own, normed, head_sems, 4, False):
         copy.start()
+    saves[1].start()
     for copy in head_copies(part, got, head_sems, 3, True):
         copy.wait()
 
@@ -1251,6 +1257,7 @@
 
     for column in range(width // 128):
         block_out[:, column * 128 : (column + 1) * 128] = spread_rows[column].astype(BF)
+    saves[0].start()
     for copy in head_copies(normed_own, normed, head_sems, 4, False):
         copy.wait()
 
@@ -1259,6 +1266,7 @@
     for piece in range(4 * rest):
         spot = (piece // (2 * rest), piece // rest % 2, piece % rest)
         out_total[spot] = value[piece * size : (piece + 1) * size].astype(BF)
+    saves[3].start()
 
     normed_t[...] = rows_of(normed).T
     value = jnp.dot(out_proj[...], normed_t[...], preferred_element_type=F32)
@@ -1275,8 +1283,13 @@
         own = jnp.concatenate([low.astype(F32), row_block(placed, SEG0)], axis=0)
         spread_blocks(heads, head, starts, own, sends)
 
-    for reduction in firsts:
+    for index in [2] + list(range(4, 4 + branches)):
+        saves[index].start()
+    for index, reduction in enumerate(firsts):
         reduction.finish_first()
+        saves[4 + branches + index].start()
+    for copy in saves:
+        copy.wait()
 
 
 def middle(heads, starts, first, backs, x_rows, cot, out_proj, up, down, gain, shift):
@@ -1292,22 +1305,23 @@
     piece = (2, rest, width // size, up.shape[1] // chunks)
     out_piece = (2, 2, rest, heads * E // size, width)
     far = [x_rows, cot, out_proj, up, down]
+    saved = [
+        jax.ShapeDtypeStruct((rows, width), BF),
+        jax.ShapeDtypeStruct((rows, width), F32),
+        jax.ShapeDtypeStruct((1, heads, ROWS_OUT, SEG0), BF),
+        jax.ShapeDtypeStruct(out_piece, BF),
+    ]
+    saved += sends + [jax.ShapeDtypeStruct(piece, BF)] * (2 * chunks)
     results = pl.pallas_call(
         partial(middle_kernel, heads),
         in_specs=[pl.BlockSpec(memory_space=pltpu.SMEM)]
         + vmem_specs(1 + len(backs) + 2)
         + [pl.BlockSpec(memory_space=pl.ANY)] * 5,
-        out_specs=vmem_specs(4 + len(sends) + 2 * chunks + 1),
-        out_shape=[
-            jax.ShapeDtypeStruct((rows, width), BF),
-            jax.ShapeDtypeStruct((rows, width), F32),
-            jax.ShapeDtypeStruct((2, width), F32),
-            jax.ShapeDtypeStruct((1, heads, ROWS_OUT, SEG0), BF),
-        ]
-        + sends
-        + [jax.ShapeDtypeStruct(piece, BF)] * (2 * chunks)
-        + [jax.ShapeDtypeStruct(out_piece, BF)],
-        scratch_shapes=[
+        out_specs=[pl.BlockSpec(memory_space=pl.ANY)] * len(saved) + vmem_specs(1),
+        out_shape=saved + [jax.ShapeDtypeStruct((2, width), F32)],
+        scratch_shapes=[pltpu.VMEM(value.shape, value.dtype) for value in saved]
+        + [pltpu.SemaphoreType.DMA((len(saved),))]
+        + [
             pltpu.VMEM((heads, E, SEG0), F32),
             pltpu.VMEM((heads, 1, SEG0), F32),
             pltpu.VMEM((heads, E, SEG0), BF),
@@ -1339,8 +1353,9 @@
         ),
         name="middle",
     )(starts, first, *backs, gain, shift, *far)
-    block_out, grad_hidden, gains_two, own_g = results[:4]
-    return block_out, grad_hidden, gains_two, own_g, results[4 : 4 + len(sends)], results[4 + len(sends) :]
+    block_out, grad_hidden, own_g, out_total = results[:4]
+    sends, halves = results[4 : 4 + len(sends)], results[4 + len(sends) : -1]
+    return block_out, grad_hidden, results[-1], own_g, sends, list(halves) + [out_total]
 
 
 def local(
@@ -1381,8 +1396,7 @@
         heads, offsets, own, own_g, units, sends_g, parts,
         normed, in_proj, x_rows, grad_hidden, first_gain, gains_two,
     )
-    results = finish([block_out, grad_tokens] + sums, [BF] + [F32] * 5)
-    return (*results, gains[0], gains[1], gains[2], gains[3])
+    return tuple(finish([block_out, grad_tokens] + sums, [BF] + [F32] * 5, gains))
 
 
 def solution(mesh):

time: 263 us -> 260 us (0.989)
  no operation moved by 1% of the time
where the time goes in v4:
time: 260 us
  Pallas kernels  256 us (98%)
    pallas_call x1, Pallas kernels, backward(): pl.pallas_call(partial(backward_kernel, heads, streams), in_specs=[pl.Blo...  138 us
    pallas_call x1, Pallas kernels, forward(): pl.pallas_call(partial(forward_kernel, heads), in_specs=[pl.BlockSpec(mem...  58.8 us
    pallas_call x1, Pallas kernels, middle(): pl.pallas_call(partial(middle_kernel, heads), in_specs=[pl.BlockSpec(memo...  50.8 us
    pallas_call x1, Pallas kernels, finish(): pl.pallas_call(finish_kernel, grid=(steps,), in_specs=[pl.BlockSpec(gains...  8.63 us

profile of v4, /device:TPU:0, one launch (start us, length us, event | category | flops | bytes accessed | tf_op | source)
XLA Modules:
  0.0 259.6 jit_solution(6553635494148496931)
XLA Ops:
  0.7 0.7 dynamic_slice.3
  1.4 0.4 reshape.125
  1.8 0.2 copy.22
  2.0 0.1 broadcast_in_dim_reshape.3
  2.1 1.4 select_convert_fusion.bits
  3.5 58.8 %forward.1 = (f32[512,768]{1,0:T(8,128)}, bf16[16,2,32,768]{3,2,1,0:T(8,128)(2,1)}, bf16[16,2,32,768]{3,2,1,0:T(8,128)(2,1)}, bf16[1,8,160,1024]{3,2,1,0:T(8,128...) custom-call(s32[5,8]{1,0:T(8,128)} %refs_0_.3, ...), custom_call_target="tpu_custom_call" | custom-call | flops 17179869184 | bytes 16384000 | tf_op jit(solution)/shard_map/forward/pallas_call | solution.py:509
  62.3 50.8 %middle.1 = (bf16[512,768]{1,0:T(8,128)(2,1)}, f32[512,768]{1,0:T(8,128)}, bf16[1,8,64,1024]{3,2,1,0:T(8,128)(2,1)}, bf16[2,2,4,24,768]{4,3,2,1,0:T(8,128)(2,1)}...) custom-call(s32[5,8]{1,0:T(8,128)} %refs_0_.3, ...), custom_call_target="tpu_custom_call" | custom-call | flops 16911433728 | bytes 41943040 | tf_op jit(solution)/shard_map/middle/pallas_call | solution.py:1315
  113.0 137.7 %backward.1 = (bf16[2,2,4,48,1536]{4,3,2,1,0:T(8,128)(2,1)}, bf16[2,2,2,4,48,768]{5,4,3,2,1,0:T(8,128)(2,1)}, bf16[2,2,4,24,768]{4,3,2,1,0:T(8,128)(2,1)}, bf16[...) custom-call(s32[5,8]{1,0:T(8,128)} %refs_0_.3, f32[768]{0:T(1024)} %refs_1_.1, ...), custom_call_target="tpu_custom_call" | custom-call | flops 42949672960 | bytes 16384000 | tf_op jit(solution)/shard_map/backward/pallas_call | solution.py:973
  250.8 8.6 %finish.1 = (bf16[512,768]{1,0:T(8,128)(2,1)}, f32[512,768]{1,0:T(8,128)}, f32[3,768,384]{2,1,0:T(8,128)}, f32[384,768]{1,0:T(8,128)}, f32[768,1536]{1,0:T(8,128...) custom-call(f32[8,768]{1,0:T(8,128)} %get-tuple-element.67.gains, ...), custom_call_target="tpu_custom_call" | custom-call | tf_op jit(solution)/shard_map/finish/pallas_call | solution.py:1047
  (3 shorter events, 0.0 us)

commit v5 on v4

--- a/solution.py
+++ b/solution.py
@@ -577,21 +577,20 @@
 
 
 ORDERS = {
-    'u1': (0, 1), 'u2': (0, 1), 'd1': (1, 0), 'd2': (1, 0), 'o': (0, 1), 'i0': (1, 0), 'i1': (1, 0), 'i2': (0,
-    1),
+    'u1': (0, 1), 'u2': (0, 1), 'd1': (1, 0), 'd2': (1, 0), 'o': (0, 1), 'i0': (1, 0), 'i1': (0, 1), 'i2': (1,
+    0),
 }
 EARLY = [
-    (0, 'd1', 0), (0, 'u1', 0), (0, 'd1', 1), (0, 'u2', 0), (0, 'u1', 1), (2, 'o', 0), (4, 'u2', 1), (5, 'u1',
-    2), (7, 'd1', 2), (9, 'u1', 3), (10, 'd2', 0), (12, 'd2', 1), (12, 'o', 1), (12, 'd1', 3), (13, 'u2', 2),
-    (14, 'u1', 4),
+    (1, 'd1', 0), (1, 'u1', 0), (2, 'd1', 1), (2, 'u1', 1), (3, 'o', 0), (6, 'u1', 2), (6, 'd2', 0), (6, 'u2',
+    0), (8, 'u2', 1), (8, 'd1', 2), (10, 'u1', 3), (12, 'd1', 3), (12, 'd2', 1), (13, 'u2', 2), (13, 'o', 1),
 ]
 TAIL = [
-    'gather', ('d1', 4), 'in1', ('i1', 0), ('d2', 2), 'in2', ('u2', 3), ('i2', 0), 'in0', ('i0', 0), ('d2',
-    3), ('i1', 1), ('i2', 1), ('u1', 5), ('u2', 4), ('d2', 4), ('d1', 5), ('o', 2), ('i2', 2), ('i0', 1),
-    ('i1', 2), ('i2', 3), 'one', ('d2', 5), ('o', 3), ('i1', 3), ('u1', 6), ('u2', 5), 'norm', ('i2', 4),
-    'gain0', ('i0', 2), ('i1', 4), ('i0', 3), 'gain1', ('o', 4), ('i0', 4), ('i2', 5), 'gain2', ('i1', 5),
-    ('o', 5), ('i0', 5), 'gain3', ('i0', 6), ('d2', 6), ('u2', 6), 'gain4', ('d1', 6), ('i1', 6), ('i2', 6),
-    ('o', 6),
+    ('u1', 4), 'gather', ('d1', 4), 'in0', ('i0', 0), ('d2', 2), 'in1', ('u1', 5), 'in2', ('i2', 0), ('i0',
+    1), ('d1', 5), ('u2', 3), ('o', 2), ('d2', 3), 'one', ('i2', 1), 'norm', ('i0', 2), ('i1', 0), ('u1', 6),
+    ('u2', 4), ('o', 3), ('d2', 4), ('i0', 3), ('i1', 1), 'gain0', ('o', 4), ('i0', 4), ('i2', 2), ('i1', 2),
+    ('d2', 5), 'gain1', ('u2', 5), ('i2', 3), ('i1', 3), ('i1', 4), ('i0', 5), 'gain2', ('i2', 4), ('o', 5),
+    ('i1', 5), ('i2', 5), ('d2', 6), 'gain3', ('i2', 6), ('u2', 6), 'gain4', ('d1', 6), ('o', 6), ('i1', 6),
+    ('i0', 6),
 ]
 
 

time: 260 us -> 260 us (level)
  no operation moved by 1% of the time
where the time goes in v5:
time: 260 us
  Pallas kernels  256 us (98%)
    pallas_call x1, Pallas kernels, backward(): pl.pallas_call(partial(backward_kernel, heads, streams), in_specs=[pl.Blo...  138 us
    pallas_call x1, Pallas kernels, forward(): pl.pallas_call(partial(forward_kernel, heads), in_specs=[pl.BlockSpec(mem...  58.8 us
    pallas_call x1, Pallas kernels, middle(): pl.pallas_call(partial(middle_kernel, heads), in_specs=[pl.BlockSpec(memo...  50.8 us
    pallas_call x1, Pallas kernels, finish(): pl.pallas_call(finish_kernel, grid=(steps,), in_specs=[pl.BlockSpec(gains...  8.63 us

profile of v5, /device:TPU:0, one launch (start us, length us, event | category | flops | bytes accessed | tf_op | source)
XLA Modules:
  0.0 259.8 jit_solution(10776553871864641503)
XLA Ops:
  0.7 0.7 dynamic_slice.3
  1.4 0.4 reshape.125
  1.8 0.2 copy.22
  2.0 0.1 broadcast_in_dim_reshape.3
  2.1 1.4 select_convert_fusion.bits
  3.5 58.8 %forward.1 = (f32[512,768]{1,0:T(8,128)}, bf16[16,2,32,768]{3,2,1,0:T(8,128)(2,1)}, bf16[16,2,32,768]{3,2,1,0:T(8,128)(2,1)}, bf16[1,8,160,1024]{3,2,1,0:T(8,128...) custom-call(s32[5,8]{1,0:T(8,128)} %refs_0_.3, ...), custom_call_target="tpu_custom_call" | custom-call | flops 17179869184 | bytes 16384000 | tf_op jit(solution)/shard_map/forward/pallas_call | solution.py:509
  62.3 50.8 %middle.1 = (bf16[512,768]{1,0:T(8,128)(2,1)}, f32[512,768]{1,0:T(8,128)}, bf16[1,8,64,1024]{3,2,1,0:T(8,128)(2,1)}, bf16[2,2,4,24,768]{4,3,2,1,0:T(8,128)(2,1)}...) custom-call(s32[5,8]{1,0:T(8,128)} %refs_0_.3, ...), custom_call_target="tpu_custom_call" | custom-call | flops 16911433728 | bytes 41943040 | tf_op jit(solution)/shard_map/middle/pallas_call | solution.py:1314
  113.0 138.0 %backward.1 = (bf16[2,2,4,48,1536]{4,3,2,1,0:T(8,128)(2,1)}, bf16[2,2,2,4,48,768]{5,4,3,2,1,0:T(8,128)(2,1)}, bf16[2,2,4,24,768]{4,3,2,1,0:T(8,128)(2,1)}, bf16[...) custom-call(s32[5,8]{1,0:T(8,128)} %refs_0_.3, f32[768]{0:T(1024)} %refs_1_.1, ...), custom_call_target="tpu_custom_call" | custom-call | flops 42949672960 | bytes 16384000 | tf_op jit(solution)/shard_map/backward/pallas_call | solution.py:972
  251.0 8.6 %finish.1 = (bf16[512,768]{1,0:T(8,128)(2,1)}, f32[512,768]{1,0:T(8,128)}, f32[3,768,384]{2,1,0:T(8,128)}, f32[384,768]{1,0:T(8,128)}, f32[768,1536]{1,0:T(8,128...) custom-call(f32[8,768]{1,0:T(8,128)} %get-tuple-element.67.gains, ...), custom_call_target="tpu_custom_call" | custom-call | tf_op jit(solution)/shard_map/finish/pallas_call | solution.py:1046
  (3 shorter events, 0.0 us)
